TPU v7x, 32 devices: a whole 2x2x4 slice. The times are simulated.
32 devices in a mesh: pair: 4 (over y, x), mat: 8 (over z, core).
Axes of the slice: x: 2, y: 2, z: 4, core: 2. Of those that a mesh axis runs over, the one named last changes fastest.
Arguments:
- operators: bfloat16 [16, 2048, 2048], P('pair', 'mat'), may hold values from -6 to 6
- left_rot: bfloat16 [2048, 2048], P('mat'), may hold values from -0.125 to 0.125
- right_rot: bfloat16 [2048, 2048], P('mat'), may hold values from -0.125 to 0.125
- integrals: float32 [1024, 1024], replicated, may hold values from -1.5 to 1.5
- pair_index: int32 [16], replicated, may hold values from 0 to 1023
- target_index: int32 [16], replicated, may hold values from 0 to 1023
Outputs:
- complement: bfloat16 [16, 2048, 2048], P('pair', None, 'mat')
All inputs are finite; a program needn't handle non-finite values.
Results may differ from a plain program's by a relative error of at most 0.0063.
Values may be sent and summed in bfloat16 or wider, within the bound.
A program may use at most 192 MiB of HBM per device.

v0:
```python
import functools

import jax
import jax.numpy as jnp
from jax import lax
from jax.experimental import pallas as pl
from jax.experimental.pallas import tpu as pltpu
from jax.sharding import PartitionSpec as P

CORES = 2
NEAR = 2
BLOCK = 16
MESH_ID = pl.DeviceIdType.MESH


def flip(index, offset, count):
    total, bit = 0, 1
    while bit < count:
        total = total + bit * ((index // bit + offset // bit) % 2)
        bit *= 2
    return total


def kernel(npair, nline, offsets, a_hbm, r_hbm, lt_hbm, kron_ref, out_hbm,
           a_ref, r_ref, lt_ref, h_ref, g_ref, x_ref, y_ref, z_ref, acc_ref, stage_ref,
           load_sem, line_send, line_recv, plane_send, plane_recv, core_send, core_recv,
           swap_send, swap_recv, in_send, in_recv, out_send, out_recv, store_sem):
    own, rows, cols = a_hbm.shape
    ntg = own
    nmat = nline * CORES
    width = cols // nmat
    strip = rows // npair
    mpiece = cols // npair
    pair, mat = lax.axis_index("pair"), lax.axis_index("mat")
    line, core = mat // CORES, mat % CORES
    peers = tuple(range(1, npair))
    straight = tuple(e for e in peers if e % NEAR == 0 or e // NEAR == 0)
    far = tuple(e for e in peers if e not in straight)

    def place(i, f):
        return flip(line, offsets(i), nline) * CORES + flip(core, f, CORES)

    def partner(e):
        return flip(pair, e, npair)

    def remote(src, dst, send, recv, pair_id, mat_id):
        return pltpu.make_async_remote_copy(
            src_ref=src, dst_ref=dst, send_sem=send, recv_sem=recv,
            device_id={"pair": pair_id, "mat": mat_id}, device_id_type=MESH_ID)

    loads = [pltpu.make_async_copy(r_hbm, r_ref.at[pl.ds(0, rows), :], load_sem.at[0]),
             pltpu.make_async_copy(lt_hbm, lt_ref.at[0, :, pl.ds(0, rows)], load_sem.at[1])]
    for s in range(nmat):
        start = pl.multiple_of(place(s // CORES, s % CORES) * rows, rows)
        loads.append(pltpu.make_async_copy(
            a_hbm.at[:, :, pl.ds(start, rows)], a_ref.at[:, :, pl.ds(s * rows, rows)], load_sem.at[2 + s]))
    for copy in loads:
        copy.start()

    barrier = pltpu.get_barrier_semaphore()
    for s in range(1, nmat):
        pl.semaphore_signal(barrier, inc=1, device_id={"pair": pair, "mat": place(s // CORES, s % CORES)},
                            device_id_type=MESH_ID)
    for e in peers:
        pl.semaphore_signal(barrier, inc=1, device_id={"pair": partner(e), "mat": mat}, device_id_type=MESH_ID)
    pl.semaphore_wait(barrier, nmat - 1 + len(peers))

    sibling = place(0, 1)

    def piece(m, i, f, origin, part=None):
        if m == 0:
            at = pl.multiple_of((i * CORES + f) * rows + origin * strip, strip)
            if part is None:
                return r_ref.at[pl.ds(at, strip), :]
            return r_ref.at[pl.ds(at, strip), pl.ds(part * (cols // 2), cols // 2)]
        at = pl.multiple_of(origin * mpiece, mpiece)
        if part is None:
            return lt_ref.at[i, pl.ds(at, mpiece), pl.ds(f * rows, rows)]
        at = pl.multiple_of(at + part * (mpiece // 2), mpiece // 2)
        return lt_ref.at[i, pl.ds(at, mpiece // 2), pl.ds(f * rows, rows)]

    def line_copy(m, i):
        if m == 0:
            src = r_hbm.at[pl.ds(pl.multiple_of(pair * strip, strip), strip), :]
        else:
            src = lt_hbm.at[pl.ds(pl.multiple_of(pair * mpiece, mpiece), mpiece), :]
        return remote(src, piece(m, i, 0, pair), line_send.at[m, i], line_recv.at[m, i], pair, place(i, 0))

    def plane_copy(m, i, to, origin, part=None):
        block = piece(m, i, 0, partner(origin), part)
        k = to ^ origin
        h = 0 if part is None else part
        return remote(block, block, plane_send.at[m, i, k, h], plane_recv.at[m, i, k, h], partner(to), mat)

    def plane_arrival(m, i, e, part=None):
        block = piece(m, i, 0, partner(e), part)
        h = 0 if part is None else part
        return remote(block, block, plane_send.at[m, i, e, h], plane_recv.at[m, i, e, h], partner(e), mat)

    def core_copy(m, i, e):
        return remote(piece(m, i, 0, partner(e)), piece(m, i, 1, partner(e)),
                      core_send.at[m, i, e], core_recv.at[m, i, e], pair, sibling)

    def core_whole(m):
        if m == 0:
            src, dst = r_hbm, r_ref.at[pl.ds(rows, rows), :]
        else:
            src, dst = lt_hbm, lt_ref.at[0, :, pl.ds(rows, rows)]
        return remote(src, dst, core_send.at[m, 0, 0], core_recv.at[m, 0, 0], pair, sibling)

    sent = []

    def launch(copy):
        copy.start()
        sent.append(copy)

    others = tuple(range(1, nline))

    def spread_first(m):
        for i in others:
            line_copy(m, i).wait_recv()
            for e in straight:
                launch(plane_copy(m, i, e, 0))
            launch(core_copy(m, i, 0))

    def spread_second(m):
        for i in others:
            for e in straight:
                plane_arrival(m, i, e).wait_recv()
                for to in straight:
                    if to ^ e in far:
                        launch(plane_copy(m, i, to, e, 0 if e < NEAR else 1))
                launch(core_copy(m, i, e))

    def spread_third(m):
        for i in others:
            for e in far:
                plane_arrival(m, i, e, 0).wait_recv()
                plane_arrival(m, i, e, 1).wait_recv()
                launch(core_copy(m, i, e))

    def spread_last(m):
        core_whole(m).wait_recv()
        for i in others:
            for e in range(npair):
                core_copy(m, i, e).wait_recv()

    for m in range(2):
        for i in others:
            launch(line_copy(m, i))
        launch(core_whole(m))

    spread_first(0)
    spread_second(0)
    spread_first(1)
    spread_third(0)
    for copy in loads:
        copy.wait()
    spread_last(0)

    def swap_copy(s, i, f):
        return remote(h_ref.at[s], g_ref.at[s], swap_send.at[s], swap_recv.at[s], pair, place(i, f))

    def half(i, f):
        start = pl.multiple_of(place(i, f) * width, width)
        block = jnp.dot(a_ref[...].reshape(own * rows, cols), r_ref[:, pl.ds(start, width)],
                        preferred_element_type=jnp.float32)
        return block.astype(jnp.bfloat16).reshape(own, rows, width)

    def rotate(s, carry):
        i, f = s // CORES, s % CORES
        h_ref[s] = half(i, f)
        swap_copy(s, i, f).start()
        return carry

    lax.fori_loop(CORES, 2 * CORES, rotate, 0)
    g_ref[0] = half(0, 0)
    lax.fori_loop(1, CORES, rotate, 0)
    lax.fori_loop(2 * CORES, nmat, rotate, 0)

    def in_copy(s, e):
        rows_of = pl.ds(pl.multiple_of(partner(e) * strip, strip), strip)
        return remote(g_ref.at[s, :, rows_of, :], x_ref.at[s, pair], in_send.at[s, e], in_recv.at[s, e],
                      partner(e), mat)

    def in_local(s):
        rows_of = pl.ds(pl.multiple_of(pair * strip, strip), strip)
        return pltpu.make_async_copy(g_ref.at[s, :, rows_of, :], x_ref.at[s, pair], in_recv.at[s, 0])

    def out_rows(s):
        at = (s % CORES) * rows + pair * strip
        return z_ref.at[s // CORES, :, pl.ds(pl.multiple_of(at, strip), strip), :]

    def out_copy(s, e):
        return remote(y_ref.at[s, partner(e)], out_rows(s), out_send.at[s, e], out_recv.at[s, e], partner(e), mat)

    def out_local(s):
        return pltpu.make_async_copy(y_ref.at[s, pair], out_rows(s), out_recv.at[s, 0])

    def enter(s):
        if s > 0:
            swap_copy(s, s // CORES, s % CORES).wait_recv()
        for e in peers[::-1]:
            launch(in_copy(s, e))
        in_local(s).start()

    def mix(s):
        for e in peers:
            in_copy(s, e).wait_recv()
        in_local(s).wait()

        def chunk(b, carry):
            at = pl.ds(pl.multiple_of(b * BLOCK, BLOCK), BLOCK)
            block = x_ref[s, :, :, at, :].reshape(npair * own * BLOCK, width)
            mixed = jnp.dot(kron_ref[...], block, preferred_element_type=jnp.float32)
            y_ref[s, :, :, at, :] = mixed.astype(jnp.bfloat16).reshape(npair, ntg, BLOCK, width)
            return carry

        lax.fori_loop(0, strip // BLOCK, chunk, 0)
        for e in peers[::-1]:
            launch(out_copy(s, e))
        out_local(s).start()

    tile = min(512, cols)

    def finish(i):
        for f in range(CORES):
            for e in peers:
                out_copy(i * CORES + f, e).wait_recv()
            out_local(i * CORES + f).wait()

        def target(n, carry):
            t, at = n // (cols // tile), pl.ds(pl.multiple_of(n % (cols // tile) * tile, tile), tile)
            part = jnp.dot(lt_ref[i, at, :], z_ref[i, t], preferred_element_type=jnp.float32)
            if i > 0:
                part = part + acc_ref[t, at, :]
            if i < nline - 1:
                acc_ref[t, at, :] = part
            else:
                stage_ref[t, at, :] = part.astype(jnp.bfloat16)
            return carry

        steps = cols // tile
        if i < nline - 1:
            lax.fori_loop(0, ntg * steps, target, 0)
        else:
            for t in range(ntg):
                lax.fori_loop(t * steps, (t + 1) * steps, target, 0)
                pltpu.make_async_copy(stage_ref.at[t], out_hbm.at[t], store_sem.at[t]).start()

    for s in range(nmat + 1):
        if s < nmat:
            enter(s)
        if s == 1:
            spread_second(1)
        if s == 3:
            spread_third(1)
            spread_last(1)
        if s > 0:
            mix(s - 1)
        if s > CORES and s % CORES == 1:
            finish((s - CORES - 1) // CORES)
    finish(nline - 1)

    for s in range(1, nmat):
        swap_copy(s, s // CORES, s % CORES).wait_send()
    for copy in sent:
        copy.wait_send()
    for t in range(ntg):
        pltpu.make_async_copy(stage_ref.at[t], out_hbm.at[t], store_sem.at[t]).wait()


def selector(indices, count):
    return (indices[:, None] == jnp.arange(count, dtype=jnp.int32)[None, :]).astype(jnp.float32)


def shards(operators, left_rot, right_rot, integrals, pair_index, target_index):
    npairs = integrals.shape[0]
    npair, nmat = lax.axis_size("pair"), lax.axis_size("mat")
    nline = nmat // CORES
    own, rows, cols = operators.shape
    width = cols // nmat
    strip = rows // npair
    ntgt, nsel = target_index.shape[0], pair_index.shape[0]
    ntg = ntgt // npair

    rowsel = jnp.dot(selector(target_index, npairs), integrals, precision=lax.Precision.HIGHEST)
    coupling = jnp.dot(
        rowsel, selector(pair_index, npairs).T, precision=lax.Precision.HIGHEST
    ).astype(jnp.bfloat16)
    kron = jnp.kron(coupling, jnp.eye(BLOCK, dtype=jnp.bfloat16))

    def offsets(i):
        if isinstance(i, int):
            return 0 if i == 0 else (nline - 1 - (i - 1) // 2 if i % 2 == 1 else i // 2)
        odd = i % 2
        return odd * (nline - 1 - (i - 1) // 2) + (1 - odd) * (i // 2)

    nslot = nmat
    bf16 = jnp.bfloat16
    dma = pltpu.SemaphoreType.DMA
    anywhere = pl.BlockSpec(memory_space=pl.ANY)
    return pl.pallas_call(
        functools.partial(kernel, npair, nline, offsets),
        out_shape=jax.ShapeDtypeStruct((ntg, cols, width), bf16),
        in_specs=[anywhere, anywhere, anywhere, pl.BlockSpec(memory_space=pltpu.VMEM)],
        out_specs=anywhere,
        scratch_shapes=[
            pltpu.VMEM((own, rows, cols), bf16),
            pltpu.VMEM((cols, cols), bf16),
            pltpu.VMEM((nline, cols, CORES * rows), bf16),
            pltpu.VMEM((nslot, own, rows, width), bf16),
            pltpu.VMEM((nslot, own, rows, width), bf16),
            pltpu.VMEM((nslot, npair, own, strip, width), bf16),
            pltpu.VMEM((nslot, npair, ntg, strip, width), bf16),
            pltpu.VMEM((nline, ntg, CORES * rows, width), bf16),
            pltpu.VMEM((ntg, cols, width), jnp.float32),
            pltpu.VMEM((ntg, cols, width), bf16),
            dma((2 + nslot,)),
            dma((2, nline)), dma((2, nline)),
            dma((2, nline, npair, 2)), dma((2, nline, npair, 2)),
            dma((2, nline, npair)), dma((2, nline, npair)),
            dma((nslot,)), dma((nslot,)),
            dma((nslot, npair)), dma((nslot, npair)),
            dma((nslot, npair)), dma((nslot, npair)),
            dma((ntg,)),
        ],
        compiler_params=pltpu.CompilerParams(
            collective_id=0, has_side_effects=True, vmem_limit_bytes=67043328),
    )(operators, right_rot, left_rot.T, kron)


def solution(mesh):
    in_specs = (P("pair", "mat", None), P("mat", None), P("mat", None), P(), P(), P())
    out_specs = P("pair", None, "mat")
    return jax.shard_map(shards, mesh=mesh, in_specs=in_specs, out_specs=out_specs, check_vma=False)
```

profile of v0, /device:TPU:0, one launch (start us, length us, event | category | flops | bytes accessed | tf_op | source)
XLA Modules:
  0.0 188.4 jit_solution(8834834547702010736)
XLA Ops:
  0.0 0.0 copy-start.1
  0.0 0.0 copy-start
  0.0 3.8 %fusion = f32[16,1024]{1,0:T(8,128)S(1)} fusion(f32[1024,1024]{1,0:T(8,128)} %param.9, s32[16]{0:T(128)} %param.11), kind=kOutput, calls=%fused_computation.4 | convolution fusion | flops 201342976 | bytes 4259904 | tf_op jit(solution)/shard_map/dot_general | solution.py:287
  3.8 0.0 copy-done.1
  3.8 0.2 convolution_convert_fusion
  4.0 0.2 broadcast_multiply_fusion
  4.2 1.6 mul.27.kron_ref
  5.8 0.0 copy-done
  5.8 1.3 copy.7
  7.1 176.8 %shard_map.64 = bf16[4,2048,256]{2,1,0:T(8,128)(2,1)} custom-call(bf16[4,256,2048]{2,1,0:T(8,128)(2,1)} %a_hbm.1, bf16[256,2048]{1,0:T(8,128)(2,1)} %r_hbm.1, bf16[2048,256]{1,0:T(8,128)(2,1)} %bitcast.5, bf16[256,256]{1,0:T(8,128)(2,1)} %mul.27.kron_ref), custom_call_target="tpu_custom_call" | custom-call | tf_op jit(solution)/shard_map/pallas_call | solution.py:303
  183.9 4.5 %copy.9 = bf16[4,2048,256]{2,1,0:T(8,128)(2,1)} copy(bf16[4,2048,256]{2,1,0:T(8,128)(2,1)} %shard_map.64) | data formatting | bytes 8388608
  (1 shorter events, 0.0 us)
Async XLA Ops:
  0.0 3.8 %copy-start.1 = (s32[16]{0:T(128)S(1)}, s32[16]{0:T(128)}, u32[]{:S(2)}) copy-start(s32[16]{0:T(128)} %param.10) | copy-start | bytes 196
  0.0 5.8 %copy-start = (bf16[256,2048]{1,0:T(8,128)(2,1)S(1)}, bf16[256,2048]{1,0:T(8,128)(2,1)}, u32[]{:S(2)}) copy-start(bf16[256,2048]{1,0:T(8,128)(2,1)} %param.7) | copy-start | bytes 3145732
where the time goes:
time: 189 us; the launch traced here: 188 us
  Pallas kernels  177 us (94%)
  local copies, waits for them, and re-layouts  7.41 us (4%)
  matrix products  3.97 us (2%)
    pallas_call x1, Pallas kernels, shards(): pl.pallas_call(functools.partial(kernel, npair, nline, offsets), out_shap...  177 us
    unnamed x6, local copies, waits for them, and re-layouts  5.78 us

commit v1 on v0

v1 whole, which is shorter than its diff:
```python
import functools

import jax
import jax.numpy as jnp
from jax import lax
from jax.experimental import pallas as pl
from jax.experimental.pallas import tpu as pltpu
from jax.sharding import PartitionSpec as P

CORES = 2
NEAR = 2
BLOCK = 16
RIGHT, LEFT = 0, 1
UP, DOWN = 0, 1
MESH_ID = pl.DeviceIdType.MESH


def flip(index, offset, count):
    total, bit = 0, 1
    while bit < count:
        total = total + bit * ((index // bit + offset // bit) % 2)
        bit *= 2
    return total


def offset_of(i, nline):
    if isinstance(i, int):
        return 0 if i == 0 else (nline - 1 - (i - 1) // 2 if i % 2 == 1 else i // 2)
    odd = i % 2
    return odd * (nline - 1 - (i - 1) // 2) + (1 - odd) * (i // 2)


def kernel(npair, nline, targets_ref, pairs_ref, a_hbm, r_hbm, l_hbm, integrals_hbm, out_hbm,
           a_ref, r_ref, l_ref, lt_ref, integrals_ref, rows_ref, kron_ref, h_ref, g_ref, x_ref, y_ref, z_ref,
           acc_ref, stage_ref,
           load_sem, line_send, line_recv, plane_send, plane_recv, core_send, core_recv,
           swap_send, swap_recv, in_send, in_recv, out_send, out_recv, store_sem):
    own, rows, cols = a_hbm.shape
    ntgt, nsel = targets_ref.shape[0], pairs_ref.shape[0]
    ntg = ntgt // npair
    nmat = nline * CORES
    width = cols // nmat
    strip = rows // npair
    mpiece = cols // npair
    pair, mat = lax.axis_index("pair"), lax.axis_index("mat")
    line, core = mat // CORES, mat % CORES
    peers = tuple(range(1, npair))
    straight = tuple(e for e in peers if e % NEAR == 0 or e // NEAR == 0)
    far = tuple(e for e in peers if e not in straight)
    hops = range(1, nline)

    def place(i, f):
        return flip(line, offset_of(i, nline), nline) * CORES + flip(core, f, CORES)

    def partner(e):
        return flip(pair, e, npair)

    sibling = line * CORES + flip(core, 1, CORES)

    def remote(src, dst, send, recv, pair_id, mat_id):
        return pltpu.make_async_remote_copy(
            src_ref=src, dst_ref=dst, send_sem=send, recv_sem=recv,
            device_id={"pair": pair_id, "mat": mat_id}, device_id_type=MESH_ID)

    sent = []

    def launch(make, cond=None):
        sent.append((make, cond))
        if cond is None:
            make().start()
        else:
            pl.when(cond)(lambda: make().start())

    load_r = pltpu.make_async_copy(r_hbm, r_ref.at[pl.ds(pl.multiple_of(mat * rows, rows), rows), :], load_sem.at[0])
    load_l = pltpu.make_async_copy(l_hbm, l_ref, load_sem.at[1])
    load_i = pltpu.make_async_copy(integrals_hbm, integrals_ref, load_sem.at[2])
    load_a = pltpu.make_async_copy(a_hbm, a_ref, load_sem.at[3])
    for copy in (load_l, load_i, load_r, load_a):
        copy.start()

    barrier = pltpu.get_barrier_semaphore()
    for s in range(1, nmat):
        pl.semaphore_signal(barrier, inc=1, device_id={"pair": pair, "mat": place(s // CORES, s % CORES)},
                            device_id_type=MESH_ID)
    for e in peers:
        pl.semaphore_signal(barrier, inc=1, device_id={"pair": partner(e), "mat": mat}, device_id_type=MESH_ID)
    pl.semaphore_wait(barrier, nmat - 1 + len(peers))

    def piece(m, source, c, origin, part=None):
        if m == RIGHT:
            at = pl.multiple_of((source * CORES + c) * rows + origin * strip, strip)
            if part is None:
                return r_ref.at[pl.ds(at, strip), :]
            return r_ref.at[pl.ds(at, strip), pl.ds(part * (cols // 2), cols // 2)]
        lanes = pl.ds(pl.multiple_of(c * rows, rows), rows)
        at = pl.multiple_of(origin * mpiece, mpiece)
        if part is None:
            return lt_ref.at[source, pl.ds(at, mpiece), lanes]
        at = pl.multiple_of(at + part * (mpiece // 2), mpiece // 2)
        return lt_ref.at[source, pl.ds(at, mpiece // 2), lanes]

    def own_piece(m):
        if m == RIGHT:
            return r_hbm.at[pl.ds(pl.multiple_of(pair * strip, strip), strip), :]
        return piece(LEFT, line, core, pair)

    def chain_copy(m, source, way, first):
        block = piece(m, source, core, pair)
        step = 1 if way == UP else -1
        return remote(own_piece(m) if first else block, block, line_send.at[m, source, way], line_recv.at[m, source],
                      pair, (line + step) * CORES + core)

    def line_copy(m, i):
        other = place(i, 0)
        return remote(own_piece(m), piece(m, line, core, pair), line_send.at[m, other // CORES, UP],
                      line_recv.at[m, line], pair, other)

    def line_arrival(m, source):
        block = piece(m, source, core, pair)
        return remote(block, block, line_send.at[m, source, UP], line_recv.at[m, source], pair, sibling)

    def plane_copy(m, source, to, origin, part=None):
        block = piece(m, source, core, partner(origin), part)
        k, h = to ^ origin, 0 if part is None else part
        return remote(block, block, plane_send.at[m, source, k, h], plane_recv.at[m, source, k, h], partner(to), mat)

    def plane_arrival(m, source, e, part=None):
        block = piece(m, source, core, partner(e), part)
        h = 0 if part is None else part
        return remote(block, block, plane_send.at[m, source, e, h], plane_recv.at[m, source, e, h], partner(e), mat)

    def core_copy(m, source, e, mine=True):
        block = piece(m, source, core if mine else flip(core, 1, CORES), partner(e))
        return remote(block, block, core_send.at[m, source, e], core_recv.at[m, source, e], pair, sibling)

    def core_whole(m):
        if m == RIGHT:
            src, dst = r_hbm, r_ref.at[pl.ds(pl.multiple_of(mat * rows, rows), rows), :]
        else:
            src = dst = lt_ref.at[line, :, pl.ds(pl.multiple_of(core * rows, rows), rows)]
        return remote(src, dst, core_send.at[m, line, 0], core_recv.at[m, line, 0], pair, sibling)

    def reaches(way, h):
        if way == UP:
            return line >= h, line - h
        return line + h < nline, line + h

    def both(h, act):
        for way in (UP, DOWN):
            cond, source = reaches(way, h)
            act(way, cond, source)

    def spread_first(m, h):
        def act(way, cond, source):
            pl.when(cond)(lambda: line_arrival(m, source).wait_recv())
            if m == RIGHT and h + 1 < nline:
                more = line < nline - 1 if way == UP else line > 0
                launch(lambda: chain_copy(m, source, way, False), cond & more)
            for e in straight:
                launch(lambda e=e: plane_copy(m, source, e, 0), cond)
            launch(lambda: core_copy(m, source, 0), cond)
        both(h, act)

    def spread_second(m, h):
        def act(way, cond, source):
            for e in straight:
                pl.when(cond)(lambda e=e: plane_arrival(m, source, e).wait_recv())
                for to in straight:
                    if to ^ e in far:
                        launch(lambda e=e, to=to: plane_copy(m, source, to, e, 0 if e < NEAR else 1), cond)
                launch(lambda e=e: core_copy(m, source, e), cond)
        both(h, act)

    def spread_third(m, h):
        def act(way, cond, source):
            for e in far:
                for part in range(2):
                    pl.when(cond)(lambda e=e, part=part: plane_arrival(m, source, e, part).wait_recv())
                launch(lambda e=e: core_copy(m, source, e), cond)
        both(h, act)

    def spread_last(m, h):
        def act(way, cond, source):
            for e in range(npair):
                pl.when(cond)(lambda e=e: core_copy(m, source, e, False).wait_recv())
        both(h, act)

    launch(lambda: chain_copy(RIGHT, line, UP, True), line < nline - 1)
    launch(lambda: chain_copy(RIGHT, line, DOWN, True), line > 0)
    launch(lambda: core_whole(RIGHT))

    load_l.wait()
    lanes = pl.ds(pl.multiple_of(core * rows, rows), rows)

    def turn(b, carry):
        at = pl.ds(pl.multiple_of(b * 256, 256), 256)
        lt_ref[line, at, lanes] = l_ref[:, at].T
        return carry

    lax.fori_loop(0, cols // 256, turn, 0)

    load_i.wait()
    for t in range(ntgt):
        rows_ref[pl.ds(t, 1), :] = integrals_ref[pl.ds(targets_ref[t], 1), :]
    picked = rows_ref[...]
    lane = lax.broadcasted_iota(jnp.int32, picked.shape, 1)
    column = lax.broadcasted_iota(jnp.int32, (ntgt, nsel), 1)
    coupling = jnp.zeros((ntgt, nsel), jnp.float32)
    for k in range(nsel):
        value = jnp.sum(jnp.where(lane == pairs_ref[k], picked, 0.0), axis=1, keepdims=True)
        coupling = jnp.where(column == k, value, coupling)
    down = lax.broadcasted_iota(jnp.int32, (ntgt * BLOCK, ntgt), 0) // BLOCK
    tall = (down == lax.broadcasted_iota(jnp.int32, (ntgt * BLOCK, ntgt), 1)).astype(jnp.bfloat16)
    across = lax.broadcasted_iota(jnp.int32, (nsel, nsel * BLOCK), 1) // BLOCK
    broad = (across == lax.broadcasted_iota(jnp.int32, (nsel, nsel * BLOCK), 0)).astype(jnp.bfloat16)
    wide = jnp.dot(coupling.astype(jnp.bfloat16), broad, preferred_element_type=jnp.float32).astype(jnp.bfloat16)
    full = jnp.dot(tall, wide, preferred_element_type=jnp.float32)
    same = (lax.broadcasted_iota(jnp.int32, full.shape, 0) % BLOCK
            == lax.broadcasted_iota(jnp.int32, full.shape, 1) % BLOCK)
    kron_ref[...] = jnp.where(same, full, 0.0).astype(jnp.bfloat16)

    for h in range(1, nline + 2):
        if h < nline:
            spread_first(RIGHT, h)
        if h == nline - 1:
            for i in hops:
                launch(lambda i=i: line_copy(LEFT, i))
            launch(lambda: core_whole(LEFT))
        if 1 <= h - 1 < nline:
            spread_second(RIGHT, h - 1)
        if 1 <= h - 2 < nline:
            spread_third(RIGHT, h - 2)
    load_r.wait()
    load_a.wait()
    core_whole(RIGHT).wait_recv()
    for h in hops:
        spread_last(RIGHT, h)

    def swap_copy(s, i, f):
        return remote(h_ref.at[s], g_ref.at[s], swap_send.at[s], swap_recv.at[s], pair, place(i, f))

    def half(i, f):
        start = pl.multiple_of(place(i, f) * width, width)
        block = jnp.dot(a_ref[...].reshape(own * rows, cols), r_ref[:, pl.ds(start, width)],
                        preferred_element_type=jnp.float32)
        return block.astype(jnp.bfloat16).reshape(own, rows, width)

    def rotate(s, carry):
        i, f = s // CORES, s % CORES
        h_ref[s] = half(i, f)
        swap_copy(s, i, f).start()
        return carry

    def in_copy(s, e):
        rows_of = pl.ds(pl.multiple_of(partner(e) * strip, strip), strip)
        return remote(g_ref.at[s, :, rows_of, :], x_ref.at[s, pair], in_send.at[s, e], in_recv.at[s, e],
                      partner(e), mat)

    def in_local(s):
        rows_of = pl.ds(pl.multiple_of(pair * strip, strip), strip)
        return pltpu.make_async_copy(g_ref.at[s, :, rows_of, :], x_ref.at[s, pair], in_recv.at[s, 0])

    def out_rows(s):
        at = flip(core, s % CORES, CORES) * rows + pair * strip
        return z_ref.at[s // CORES, :, pl.ds(pl.multiple_of(at, strip), strip), :]

    def out_copy(s, e):
        return remote(y_ref.at[s, partner(e)], out_rows(s), out_send.at[s, e], out_recv.at[s, e], partner(e), mat)

    def out_local(s):
        return pltpu.make_async_copy(y_ref.at[s, pair], out_rows(s), out_recv.at[s, 0])

    def enter(s):
        if s > 0:
            swap_copy(s, s // CORES, s % CORES).wait_recv()
        for e in peers[::-1]:
            launch(lambda e=e: in_copy(s, e))
        in_local(s).start()

    def mix(s):
        for e in peers:
            in_copy(s, e).wait_recv()
        in_local(s).wait()

        def chunk(b, carry):
            at = pl.ds(pl.multiple_of(b * BLOCK, BLOCK), BLOCK)
            block = x_ref[s, :, :, at, :].reshape(npair * own * BLOCK, width)
            mixed = jnp.dot(kron_ref[...], block, preferred_element_type=jnp.float32)
            y_ref[s, :, :, at, :] = mixed.astype(jnp.bfloat16).reshape(npair, ntg, BLOCK, width)
            return carry

        lax.fori_loop(0, strip // BLOCK, chunk, 0)
        for e in peers[::-1]:
            launch(lambda e=e: out_copy(s, e))
        out_local(s).start()

    tile = min(512, cols)

    def finish(i):
        for f in range(CORES):
            for e in peers:
                out_copy(i * CORES + f, e).wait_recv()
            out_local(i * CORES + f).wait()
        source = flip(line, offset_of(i, nline), nline)

        def target(n, carry):
            t, at = n // (cols // tile), pl.ds(pl.multiple_of(n % (cols // tile) * tile, tile), tile)
            part = jnp.dot(lt_ref[source, at, :], z_ref[i, t], preferred_element_type=jnp.float32)
            if i > 0:
                part = part + acc_ref[t, at, :]
            if i < nline - 1:
                acc_ref[t, at, :] = part
            else:
                stage_ref[t, at, :] = part.astype(jnp.bfloat16)
            return carry

        steps = cols // tile
        if i < nline - 1:
            lax.fori_loop(0, ntg * steps, target, 0)
        else:
            for t in range(ntg):
                lax.fori_loop(t * steps, (t + 1) * steps, target, 0)
                pltpu.make_async_copy(stage_ref.at[t], out_hbm.at[t], store_sem.at[t]).start()

    lax.fori_loop(CORES, CORES + 1, rotate, 0)
    g_ref[0] = half(0, 0)
    enter(0)
    lax.fori_loop(CORES + 1, 2 * CORES, rotate, 0)
    lax.fori_loop(1, CORES, rotate, 0)
    enter(1)
    for h in hops:
        spread_first(LEFT, h)
    lax.fori_loop(2 * CORES, nmat, rotate, 0)

    for i in range(nline):
        first = i * CORES
        if i > 0:
            for f in range(CORES):
                enter(first + f)
        for f in range(CORES):
            mix(first + f)
            if i == 0:
                for h in hops:
                    (spread_second if f == 0 else spread_third)(LEFT, h)
        if i == 1:
            core_whole(LEFT).wait_recv()
            for h in hops:
                spread_last(LEFT, h)
        if i > 0:
            finish(i - 1)
    finish(nline - 1)

    for s in range(1, nmat):
        swap_copy(s, s // CORES, s % CORES).wait_send()
    for make, cond in sent:
        if cond is None:
            make().wait_send()
        else:
            pl.when(cond)(lambda make=make: make().wait_send())
    for t in range(ntg):
        pltpu.make_async_copy(stage_ref.at[t], out_hbm.at[t], store_sem.at[t]).wait()


def shards(operators, left_rot, right_rot, integrals, pair_index, target_index):
    npair, nmat = lax.axis_size("pair"), lax.axis_size("mat")
    nline = nmat // CORES
    own, rows, cols = operators.shape
    width = cols // nmat
    strip = rows // npair
    ntgt, nsel = target_index.shape[0], pair_index.shape[0]
    ntg = ntgt // npair
    bf16, f32 = jnp.bfloat16, jnp.float32
    dma = pltpu.SemaphoreType.DMA
    anywhere = pl.BlockSpec(memory_space=pl.ANY)
    scalars = pl.BlockSpec(memory_space=pltpu.SMEM)
    return pl.pallas_call(
        functools.partial(kernel, npair, nline),
        out_shape=jax.ShapeDtypeStruct((ntg, cols, width), bf16),
        in_specs=[scalars, scalars, anywhere, anywhere, anywhere, anywhere],
        out_specs=anywhere,
        scratch_shapes=[
            pltpu.VMEM((own, rows, cols), bf16),
            pltpu.VMEM((cols, cols), bf16),
            pltpu.VMEM((rows, cols), bf16),
            pltpu.VMEM((nline, cols, CORES * rows), bf16),
            pltpu.VMEM(integrals.shape, f32),
            pltpu.VMEM((ntgt, integrals.shape[1]), f32),
            pltpu.VMEM((ntgt * BLOCK, nsel * BLOCK), bf16),
            pltpu.VMEM((nmat, own, rows, width), bf16),
            pltpu.VMEM((nmat, own, rows, width), bf16),
            pltpu.VMEM((nmat, npair, own, strip, width), bf16),
            pltpu.VMEM((nmat, npair, ntg, strip, width), bf16),
            pltpu.VMEM((nline, ntg, CORES * rows, width), bf16),
            pltpu.VMEM((ntg, cols, width), f32),
            pltpu.VMEM((ntg, cols, width), bf16),
            dma((4,)),
            dma((2, nline, 2)), dma((2, nline)),
            dma((2, nline, npair, 2)), dma((2, nline, npair, 2)),
            dma((2, nline, npair)), dma((2, nline, npair)),
            dma((nmat,)), dma((nmat,)),
            dma((nmat, npair)), dma((nmat, npair)),
            dma((nmat, npair)), dma((nmat, npair)),
            dma((ntg,)),
        ],
        compiler_params=pltpu.CompilerParams(
            collective_id=0, has_side_effects=True, vmem_limit_bytes=67043328),
    )(target_index, pair_index, operators, right_rot, left_rot, integrals)


def solution(mesh):
    in_specs = (P("pair", "mat", None), P("mat", None), P("mat", None), P(), P(), P())
    out_specs = P("pair", None, "mat")
    return jax.shard_map(shards, mesh=mesh, in_specs=in_specs, out_specs=out_specs, check_vma=False)
```

time: 189 us -> 192 us (1.016)
  the two profiles are of different devices: /device:TPU:0 before, /device:TPU:21 now
where the time goes in v1:
time: 192 us
  Pallas kernels  187 us (97%)
  local copies, waits for them, and re-layouts  4.47 us (2%)
    pallas_call x1, Pallas kernels, shards(): pl.pallas_call(functools.partial(kernel, npair, nline), out_shape=jax.Sha...  187 us
    unnamed x1, local copies, waits for them, and re-layouts  4.47 us

profile of v1, /device:TPU:21, one launch (start us, length us, event | category | flops | bytes accessed | tf_op | source)
XLA Modules:
  0.0 191.6 jit_solution(3163297261046417422)
XLA Ops:
  0.0 187.1 %shard_map.64 = bf16[4,2048,256]{2,1,0:T(8,128)(2,1)} custom-call(s32[16]{0:T(128)} %targets_ref.1, s32[16]{0:T(128)} %pairs_ref.1, bf16[4,256,2048]{2,1,0:T(8,128)(2,1)} %a_hbm.1, bf16[256,2048]{1,0:T(8,128)(2,1)} %r_hbm.1, bf16[256,2048]{1,0:T(8,128)(2,1)} %l_hbm.1, f32[1024,1024]{1,0:T(8,128)} %integrals_hbm.1), custom_call_target="tpu_custom_call" | custom-call | tf_op jit(solution)/shard_map/pallas_call | solution.py:376
  187.1 4.5 %copy.8 = bf16[4,2048,256]{2,1,0:T(8,128)(2,1)} copy(bf16[4,2048,256]{2,1,0:T(8,128)(2,1)} %shard_map.64) | data formatting | bytes 8388608

commit v2 on v1

--- a/solution.py
+++ b/solution.py
@@ -30,17 +30,24 @@
     return odd * (nline - 1 - (i - 1) // 2) + (1 - odd) * (i // 2)
 
 
+def early_rows(own, ntg, strip):
+    return BLOCK if own == ntg and strip > BLOCK else 0
+
+
 def kernel(npair, nline, targets_ref, pairs_ref, a_hbm, r_hbm, l_hbm, integrals_hbm, out_hbm,
-           a_ref, r_ref, l_ref, lt_ref, integrals_ref, rows_ref, kron_ref, h_ref, g_ref, x_ref, y_ref, z_ref,
+           a_ref, early_ref, r_ref, l_ref, lt_ref, integrals_ref, rows_ref, kron_ref, h_ref, g_ref, x_ref, y_ref, z_ref,
            acc_ref, stage_ref,
            load_sem, line_send, line_recv, plane_send, plane_recv, core_send, core_recv,
-           swap_send, swap_recv, in_send, in_recv, out_send, out_recv, store_sem):
-    own, rows, cols = a_hbm.shape
+           swap_send, swap_recv, first_send, first_recv, in_send, in_recv, pass_send, pass_recv, out_send, out_recv,
+           store_sem):
+    own, _, strip, cols = a_hbm.shape
+    rows = npair * strip
     ntgt, nsel = targets_ref.shape[0], pairs_ref.shape[0]
     ntg = ntgt // npair
     nmat = nline * CORES
     width = cols // nmat
-    strip = rows // npair
+    early = early_rows(own, ntg, strip)
+    late = strip - early
     mpiece = cols // npair
     pair, mat = lax.axis_index("pair"), lax.axis_index("mat")
     line, core = mat // CORES, mat % CORES
@@ -110,11 +117,6 @@
         return remote(own_piece(m) if first else block, block, line_send.at[m, source, way], line_recv.at[m, source],
                       pair, (line + step) * CORES + core)
 
-    def line_copy(m, i):
-        other = place(i, 0)
-        return remote(own_piece(m), piece(m, line, core, pair), line_send.at[m, other // CORES, UP],
-                      line_recv.at[m, line], pair, other)
-
     def line_arrival(m, source):
         block = piece(m, source, core, pair)
         return remote(block, block, line_send.at[m, source, UP], line_recv.at[m, source], pair, sibling)
@@ -150,12 +152,16 @@
             cond, source = reaches(way, h)
             act(way, cond, source)
 
+    def hop(m, h):
+        def act(way, cond, source):
+            pl.when(cond)(lambda: line_arrival(m, source).wait_recv())
+            if h + 1 < nline:
+                more = line < nline - 1 if way == UP else line > 0
+                launch(lambda: chain_copy(m, source, way, False), cond & more)
+        both(h, act)
+
     def spread_first(m, h):
         def act(way, cond, source):
-            pl.when(cond)(lambda: line_arrival(m, source).wait_recv())
-            if m == RIGHT and h + 1 < nline:
-                more = line < nline - 1 if way == UP else line > 0
-                launch(lambda: chain_copy(m, source, way, False), cond & more)
             for e in straight:
                 launch(lambda e=e: plane_copy(m, source, e, 0), cond)
             launch(lambda: core_copy(m, source, 0), cond)
@@ -185,9 +191,42 @@
                 pl.when(cond)(lambda e=e: core_copy(m, source, e, False).wait_recv())
         both(h, act)
 
-    launch(lambda: chain_copy(RIGHT, line, UP, True), line < nline - 1)
-    launch(lambda: chain_copy(RIGHT, line, DOWN, True), line > 0)
-    launch(lambda: core_whole(RIGHT))
+    def depart(m):
+        launch(lambda: chain_copy(m, line, UP, True), line < nline - 1)
+        launch(lambda: chain_copy(m, line, DOWN, True), line > 0)
+        launch(lambda: core_whole(m))
+
+    def early_source(position):
+        return a_hbm.at[:, position, pl.ds(0, early), :]
+
+    def early_copy(e):
+        return remote(early_source(partner(e)), early_ref.at[pair], first_send.at[e], first_recv.at[e],
+                      partner(e), mat)
+
+    def early_mix():
+        for e in peers:
+            early_copy(e).wait_recv()
+        early_local.wait()
+        load_a.wait()
+        span = min(512, cols)
+
+        def columns(b, carry):
+            at = pl.ds(pl.multiple_of(b * span, span), span)
+            mixed = jnp.dot(kron_ref[...], early_ref[:, :, :, at].reshape(nsel * BLOCK, span),
+                            preferred_element_type=jnp.float32)
+            mixed = mixed.astype(jnp.bfloat16).reshape(npair, ntg, BLOCK, span)
+            for position in range(npair):
+                a_ref[:, position, pl.ds(0, early), at] = mixed[position]
+            return carry
+
+        lax.fori_loop(0, cols // span, columns, 0)
+
+    depart(RIGHT)
+    if early:
+        for e in peers[::-1]:
+            launch(lambda e=e: early_copy(e))
+        early_local = pltpu.make_async_copy(early_source(pair), early_ref.at[pair], first_recv.at[0])
+        early_local.start()
 
     load_l.wait()
     lanes = pl.ds(pl.multiple_of(core * rows, rows), rows)
@@ -219,19 +258,25 @@
             == lax.broadcasted_iota(jnp.int32, full.shape, 1) % BLOCK)
     kron_ref[...] = jnp.where(same, full, 0.0).astype(jnp.bfloat16)
 
+    def right(stage, h):
+        if 1 <= h < nline:
+            if stage is spread_first:
+                hop(RIGHT, h)
+            stage(RIGHT, h)
+
     for h in range(1, nline + 2):
-        if h < nline:
-            spread_first(RIGHT, h)
-        if h == nline - 1:
-            for i in hops:
-                launch(lambda i=i: line_copy(LEFT, i))
-            launch(lambda: core_whole(LEFT))
-        if 1 <= h - 1 < nline:
-            spread_second(RIGHT, h - 1)
-        if 1 <= h - 2 < nline:
-            spread_third(RIGHT, h - 2)
+        right(spread_first, h)
+        if h == 2:
+            depart(LEFT)
+        if h == 2 and early:
+            early_mix()
+        right(spread_second, h - 1)
+        if 1 <= h - 2 < nline - 1:
+            hop(LEFT, h - 2)
+        right(spread_third, h - 2)
     load_r.wait()
-    load_a.wait()
+    if not early:
+        load_a.wait()
     core_whole(RIGHT).wait_recv()
     for h in hops:
         spread_last(RIGHT, h)
@@ -243,7 +288,7 @@
         start = pl.multiple_of(place(i, f) * width, width)
         block = jnp.dot(a_ref[...].reshape(own * rows, cols), r_ref[:, pl.ds(start, width)],
                         preferred_element_type=jnp.float32)
-        return block.astype(jnp.bfloat16).reshape(own, rows, width)
+        return block.astype(jnp.bfloat16).reshape(own, npair, strip, width)
 
     def rotate(s, carry):
         i, f = s // CORES, s % CORES
@@ -251,24 +296,33 @@
         swap_copy(s, i, f).start()
         return carry
 
+    def in_rows(s, position):
+        return g_ref.at[s, :, position, pl.ds(early, late), :]
+
     def in_copy(s, e):
-        rows_of = pl.ds(pl.multiple_of(partner(e) * strip, strip), strip)
-        return remote(g_ref.at[s, :, rows_of, :], x_ref.at[s, pair], in_send.at[s, e], in_recv.at[s, e],
+        return remote(in_rows(s, partner(e)), x_ref.at[s, pair], in_send.at[s, e], in_recv.at[s, e], partner(e), mat)
+
+    def in_local(s):
+        return pltpu.make_async_copy(in_rows(s, pair), x_ref.at[s, pair], in_recv.at[s, 0])
+
+    def out_rows(s, start, count):
+        at = flip(core, s % CORES, CORES) * rows + pair * strip + start
+        return z_ref.at[s // CORES, :, pl.ds(pl.multiple_of(at, BLOCK), count), :]
+
+    def pass_copy(s, e):
+        return remote(g_ref.at[s, :, partner(e), pl.ds(0, early), :], out_rows(s, 0, early),
+                      pass_send.at[s, e], pass_recv.at[s, e], partner(e), mat)
+
+    def pass_local(s):
+        return pltpu.make_async_copy(g_ref.at[s, :, pair, pl.ds(0, early), :], out_rows(s, 0, early),
+                                     pass_recv.at[s, 0])
+
+    def out_copy(s, e):
+        return remote(y_ref.at[s, partner(e)], out_rows(s, early, late), out_send.at[s, e], out_recv.at[s, e],
                       partner(e), mat)
 
-    def in_local(s):
-        rows_of = pl.ds(pl.multiple_of(pair * strip, strip), strip)
-        return pltpu.make_async_copy(g_ref.at[s, :, rows_of, :], x_ref.at[s, pair], in_recv.at[s, 0])
-
-    def out_rows(s):
-        at = flip(core, s % CORES, CORES) * rows + pair * strip
-        return z_ref.at[s // CORES, :, pl.ds(pl.multiple_of(at, strip), strip), :]
-
-    def out_copy(s, e):
-        return remote(y_ref.at[s, partner(e)], out_rows(s), out_send.at[s, e], out_recv.at[s, e], partner(e), mat)
-
     def out_local(s):
-        return pltpu.make_async_copy(y_ref.at[s, pair], out_rows(s), out_recv.at[s, 0])
+        return pltpu.make_async_copy(y_ref.at[s, pair], out_rows(s, early, late), out_recv.at[s, 0])
 
     def enter(s):
         if s > 0:
@@ -276,6 +330,10 @@
         for e in peers[::-1]:
             launch(lambda e=e: in_copy(s, e))
         in_local(s).start()
+        if early:
+            for e in peers[::-1]:
+                launch(lambda e=e: pass_copy(s, e))
+            pass_local(s).start()
 
     def mix(s):
         for e in peers:
@@ -284,12 +342,12 @@
 
         def chunk(b, carry):
             at = pl.ds(pl.multiple_of(b * BLOCK, BLOCK), BLOCK)
-            block = x_ref[s, :, :, at, :].reshape(npair * own * BLOCK, width)
+            block = x_ref[s, :, :, at, :].reshape(nsel * BLOCK, width)
             mixed = jnp.dot(kron_ref[...], block, preferred_element_type=jnp.float32)
             y_ref[s, :, :, at, :] = mixed.astype(jnp.bfloat16).reshape(npair, ntg, BLOCK, width)
             return carry
 
-        lax.fori_loop(0, strip // BLOCK, chunk, 0)
+        lax.fori_loop(0, late // BLOCK, chunk, 0)
         for e in peers[::-1]:
             launch(lambda e=e: out_copy(s, e))
         out_local(s).start()
@@ -301,6 +359,10 @@
             for e in peers:
                 out_copy(i * CORES + f, e).wait_recv()
             out_local(i * CORES + f).wait()
+            if early:
+                for e in peers:
+                    pass_copy(i * CORES + f, e).wait_recv()
+                pass_local(i * CORES + f).wait()
         source = flip(line, offset_of(i, nline), nline)
 
         def target(n, carry):
@@ -322,14 +384,14 @@
                 lax.fori_loop(t * steps, (t + 1) * steps, target, 0)
                 pltpu.make_async_copy(stage_ref.at[t], out_hbm.at[t], store_sem.at[t]).start()
 
-    lax.fori_loop(CORES, CORES + 1, rotate, 0)
+    lax.fori_loop(CORES, 2 * CORES, rotate, 0)
     g_ref[0] = half(0, 0)
     enter(0)
-    lax.fori_loop(CORES + 1, 2 * CORES, rotate, 0)
     lax.fori_loop(1, CORES, rotate, 0)
-    enter(1)
+    hop(LEFT, nline - 1)
     for h in hops:
         spread_first(LEFT, h)
+    enter(1)
     lax.fori_loop(2 * CORES, nmat, rotate, 0)
 
     for i in range(nline):
@@ -367,6 +429,7 @@
     own, rows, cols = operators.shape
     width = cols // nmat
     strip = rows // npair
+    early = early_rows(own, target_index.shape[0] // npair, strip)
     ntgt, nsel = target_index.shape[0], pair_index.shape[0]
     ntg = ntgt // npair
     bf16, f32 = jnp.bfloat16, jnp.float32
@@ -379,17 +442,18 @@
         in_specs=[scalars, scalars, anywhere, anywhere, anywhere, anywhere],
         out_specs=anywhere,
         scratch_shapes=[
-            pltpu.VMEM((own, rows, cols), bf16),
+            pltpu.VMEM((own, npair, strip, cols), bf16),
+            pltpu.VMEM((npair, own, BLOCK, cols), bf16),
             pltpu.VMEM((cols, cols), bf16),
             pltpu.VMEM((rows, cols), bf16),
             pltpu.VMEM((nline, cols, CORES * rows), bf16),
             pltpu.VMEM(integrals.shape, f32),
             pltpu.VMEM((ntgt, integrals.shape[1]), f32),
             pltpu.VMEM((ntgt * BLOCK, nsel * BLOCK), bf16),
-            pltpu.VMEM((nmat, own, rows, width), bf16),
-            pltpu.VMEM((nmat, own, rows, width), bf16),
-            pltpu.VMEM((nmat, npair, own, strip, width), bf16),
-            pltpu.VMEM((nmat, npair, ntg, strip, width), bf16),
+            pltpu.VMEM((nmat, own, npair, strip, width), bf16),
+            pltpu.VMEM((nmat, own, npair, strip, width), bf16),
+            pltpu.VMEM((nmat, npair, own, strip - early, width), bf16),
+            pltpu.VMEM((nmat, npair, ntg, strip - early, width), bf16),
             pltpu.VMEM((nline, ntg, CORES * rows, width), bf16),
             pltpu.VMEM((ntg, cols, width), f32),
             pltpu.VMEM((ntg, cols, width), bf16),
@@ -398,13 +462,15 @@
             dma((2, nline, npair, 2)), dma((2, nline, npair, 2)),
             dma((2, nline, npair)), dma((2, nline, npair)),
             dma((nmat,)), dma((nmat,)),
+            dma((npair,)), dma((npair,)),
+            dma((nmat, npair)), dma((nmat, npair)),
             dma((nmat, npair)), dma((nmat, npair)),
             dma((nmat, npair)), dma((nmat, npair)),
             dma((ntg,)),
         ],
         compiler_params=pltpu.CompilerParams(
             collective_id=0, has_side_effects=True, vmem_limit_bytes=67043328),
-    )(target_index, pair_index, operators, right_rot, left_rot, integrals)
+    )(target_index, pair_index, operators.reshape(own, npair, strip, cols), right_rot, left_rot, integrals)
 
 
 def solution(mesh):

time: 192 us -> 177 us (0.922)
  the two profiles are of different devices: /device:TPU:21 before, /device:TPU:0 now
where the time goes in v2:
time: 177 us
  Pallas kernels  172 us (97%)
  local copies, waits for them, and re-layouts  4.47 us (3%)
    pallas_call x1, Pallas kernels, shards(): pl.pallas_call(functools.partial(kernel, npair, nline), out_shape=jax.Sha...  172 us
    unnamed x1, local copies, waits for them, and re-layouts  4.47 us

profile of v2, /device:TPU:0, one launch (start us, length us, event | category | flops | bytes accessed | tf_op | source)
XLA Modules:
  0.0 176.8 jit_solution(8323880202958226889)
XLA Ops:
  0.0 172.3 %shard_map.64 = bf16[4,2048,256]{2,1,0:T(8,128)(2,1)} custom-call(s32[16]{0:T(128)} %targets_ref.1, s32[16]{0:T(128)} %pairs_ref.1, bf16[4,4,64,2048]{3,2,1,0:T(8,128)(2,1)} %bitcast.1, bf16[256,2048]{1,0:T(8,128)(2,1)} %r_hbm.1, bf16[256,2048]{1,0:T(8,128)(2,1)} %l_hbm.1, f32[1024,1024]{1,0:T(8,128)} %integrals_hbm.1), custom_call_target="tpu_custom_call" | custom-call | tf_op jit(solution)/shard_map/pallas_call | solution.py:439
  172.3 4.5 %copy.8 = bf16[4,2048,256]{2,1,0:T(8,128)(2,1)} copy(bf16[4,2048,256]{2,1,0:T(8,128)(2,1)} %shard_map.64) | data formatting | bytes 8388608

commit v3 on v2

--- a/solution.py
+++ b/solution.py
@@ -270,9 +270,12 @@
             depart(LEFT)
         if h == 2 and early:
             early_mix()
-        right(spread_second, h - 1)
         if 1 <= h - 2 < nline - 1:
             hop(LEFT, h - 2)
+        right(spread_second, h - 1)
+        if h == nline:
+            for k in range(1, nline - 1):
+                spread_first(LEFT, k)
         right(spread_third, h - 2)
     load_r.wait()
     if not early:
@@ -354,43 +357,58 @@
 
     tile = min(512, cols)
 
+    def arrived(s):
+        for e in peers:
+            out_copy(s, e).wait_recv()
+        out_local(s).wait()
+        if early:
+            for e in peers:
+                pass_copy(s, e).wait_recv()
+            pass_local(s).wait()
+
+    steps = cols // tile
+
+    def product(i, f, add, last):
+        source = flip(line, offset_of(i, nline), nline)
+        if f is None:
+            depth = pl.ds(0, CORES * rows)
+        else:
+            depth = pl.ds(pl.multiple_of(flip(core, f, CORES) * rows, rows), rows)
+
+        def target(n, carry):
+            t, at = n // steps, pl.ds(pl.multiple_of(n % steps * tile, tile), tile)
+            part = jnp.dot(lt_ref[source, at, depth], z_ref[i, t, depth, :], preferred_element_type=jnp.float32)
+            if add:
+                part = part + acc_ref[t, at, :]
+            if last:
+                stage_ref[t, at, :] = part.astype(jnp.bfloat16)
+            else:
+                acc_ref[t, at, :] = part
+            return carry
+
+        return target
+
     def finish(i):
         for f in range(CORES):
-            for e in peers:
-                out_copy(i * CORES + f, e).wait_recv()
-            out_local(i * CORES + f).wait()
-            if early:
-                for e in peers:
-                    pass_copy(i * CORES + f, e).wait_recv()
-                pass_local(i * CORES + f).wait()
-        source = flip(line, offset_of(i, nline), nline)
-
-        def target(n, carry):
-            t, at = n // (cols // tile), pl.ds(pl.multiple_of(n % (cols // tile) * tile, tile), tile)
-            part = jnp.dot(lt_ref[source, at, :], z_ref[i, t], preferred_element_type=jnp.float32)
-            if i > 0:
-                part = part + acc_ref[t, at, :]
-            if i < nline - 1:
-                acc_ref[t, at, :] = part
-            else:
-                stage_ref[t, at, :] = part.astype(jnp.bfloat16)
-            return carry
-
-        steps = cols // tile
-        if i < nline - 1:
-            lax.fori_loop(0, ntg * steps, target, 0)
-        else:
-            for t in range(ntg):
-                lax.fori_loop(t * steps, (t + 1) * steps, target, 0)
-                pltpu.make_async_copy(stage_ref.at[t], out_hbm.at[t], store_sem.at[t]).start()
+            arrived(i * CORES + f)
+        lax.fori_loop(0, ntg * steps, product(i, None, i > 0, False), 0)
+
+    def finish_last():
+        i = nline - 1
+        for f in range(CORES):
+            arrived(i * CORES + f)
+            if f < CORES - 1:
+                lax.fori_loop(0, ntg * steps, product(i, f, i + f > 0, False), 0)
+        for t in range(ntg):
+            lax.fori_loop(t * steps, (t + 1) * steps, product(i, CORES - 1, True, True), 0)
+            pltpu.make_async_copy(stage_ref.at[t], out_hbm.at[t], store_sem.at[t]).start()
 
     lax.fori_loop(CORES, 2 * CORES, rotate, 0)
     g_ref[0] = half(0, 0)
     enter(0)
     lax.fori_loop(1, CORES, rotate, 0)
     hop(LEFT, nline - 1)
-    for h in hops:
-        spread_first(LEFT, h)
+    spread_first(LEFT, nline - 1)
     enter(1)
     lax.fori_loop(2 * CORES, nmat, rotate, 0)
 
@@ -410,7 +428,7 @@
                 spread_last(LEFT, h)
         if i > 0:
             finish(i - 1)
-    finish(nline - 1)
+    finish_last()
 
     for s in range(1, nmat):
         swap_copy(s, s // CORES, s % CORES).wait_send()

time: 177 us -> 169 us (0.955)
  Pallas kernels: 172 us -> 165 us
    pallas_call x1, Pallas kernels: 172 us -> 165 us  [shards(): pl.pallas_call(functools.partial(kernel, npair, nline), out_shape=jax.Sha...]
where the time goes in v3:
time: 169 us
  Pallas kernels  165 us (98%)
  local copies, waits for them, and re-layouts  4.47 us (3%)
    pallas_call x1, Pallas kernels, shards(): pl.pallas_call(functools.partial(kernel, npair, nline), out_shape=jax.Sha...  165 us
    unnamed x1, local copies, waits for them, and re-layouts  4.47 us

profile of v3, /device:TPU:0, one launch (start us, length us, event | category | flops | bytes accessed | tf_op | source)
XLA Modules:
  0.0 169.0 jit_solution(14015398344656641660)
XLA Ops:
  0.0 164.5 %shard_map.64 = bf16[4,2048,256]{2,1,0:T(8,128)(2,1)} custom-call(s32[16]{0:T(128)} %targets_ref.1, s32[16]{0:T(128)} %pairs_ref.1, bf16[4,4,64,2048]{3,2,1,0:T(8,128)(2,1)} %bitcast.1, bf16[256,2048]{1,0:T(8,128)(2,1)} %r_hbm.1, bf16[256,2048]{1,0:T(8,128)(2,1)} %l_hbm.1, f32[1024,1024]{1,0:T(8,128)} %integrals_hbm.1), custom_call_target="tpu_custom_call" | custom-call | tf_op jit(solution)/shard_map/pallas_call | solution.py:457
  164.5 4.5 %copy.8 = bf16[4,2048,256]{2,1,0:T(8,128)(2,1)} copy(bf16[4,2048,256]{2,1,0:T(8,128)(2,1)} %shard_map.64) | data formatting | bytes 8388608

commit v4 on v3

--- a/solution.py
+++ b/solution.py
@@ -10,7 +10,7 @@
 CORES = 2
 NEAR = 2
 BLOCK = 16
-RIGHT, LEFT = 0, 1
+LEFT = 2
 UP, DOWN = 0, 1
 MESH_ID = pl.DeviceIdType.MESH
 
@@ -34,12 +34,11 @@
     return BLOCK if own == ntg and strip > BLOCK else 0
 
 
-def kernel(npair, nline, targets_ref, pairs_ref, a_hbm, r_hbm, l_hbm, integrals_hbm, out_hbm,
+def kernel(npair, nline, targets_ref, pairs_ref, a_hbm, r_hbm, l_hbm, integrals_hbm, stage_ref,
            a_ref, early_ref, r_ref, l_ref, lt_ref, integrals_ref, rows_ref, kron_ref, h_ref, g_ref, x_ref, y_ref, z_ref,
-           acc_ref, stage_ref,
-           load_sem, line_send, line_recv, plane_send, plane_recv, core_send, core_recv,
-           swap_send, swap_recv, first_send, first_recv, in_send, in_recv, pass_send, pass_recv, out_send, out_recv,
-           store_sem):
+           acc_ref,
+           load_sem, line_send, line_recv, plane_send, plane_recv, core_send, core_recv, whole_send, whole_recv,
+           swap_send, swap_recv, first_send, first_recv, in_send, in_recv, pass_send, out_send, out_recv):
     own, _, strip, cols = a_hbm.shape
     rows = npair * strip
     ntgt, nsel = targets_ref.shape[0], pairs_ref.shape[0]
@@ -69,14 +68,16 @@
             src_ref=src, dst_ref=dst, send_sem=send, recv_sem=recv,
             device_id={"pair": pair_id, "mat": mat_id}, device_id_type=MESH_ID)
 
-    sent = []
-
     def launch(make, cond=None):
-        sent.append((make, cond))
         if cond is None:
             make().start()
         else:
             pl.when(cond)(lambda: make().start())
+
+    def await_bytes(block, sem):
+        pltpu.make_async_copy(block, block, sem).wait()
+
+    chained = []
 
     load_r = pltpu.make_async_copy(r_hbm, r_ref.at[pl.ds(pl.multiple_of(mat * rows, rows), rows), :], load_sem.at[0])
     load_l = pltpu.make_async_copy(l_hbm, l_ref, load_sem.at[1])
@@ -94,11 +95,11 @@
     pl.semaphore_wait(barrier, nmat - 1 + len(peers))
 
     def piece(m, source, c, origin, part=None):
-        if m == RIGHT:
+        if m is not LEFT:
             at = pl.multiple_of((source * CORES + c) * rows + origin * strip, strip)
-            if part is None:
-                return r_ref.at[pl.ds(at, strip), :]
-            return r_ref.at[pl.ds(at, strip), pl.ds(part * (cols // 2), cols // 2)]
+            size = cols // 2 if part is None else cols // 4
+            start = m * (cols // 2) + (0 if part is None else part * size)
+            return r_ref.at[pl.ds(at, strip), pl.ds(pl.multiple_of(start, size), size)]
         lanes = pl.ds(pl.multiple_of(c * rows, rows), rows)
         at = pl.multiple_of(origin * mpiece, mpiece)
         if part is None:
@@ -107,8 +108,8 @@
         return lt_ref.at[source, pl.ds(at, mpiece // 2), lanes]
 
     def own_piece(m):
-        if m == RIGHT:
-            return r_hbm.at[pl.ds(pl.multiple_of(pair * strip, strip), strip), :]
+        if m is not LEFT:
+            return r_hbm.at[pl.ds(pl.multiple_of(pair * strip, strip), strip), pl.ds(m * (cols // 2), cols // 2)]
         return piece(LEFT, line, core, pair)
 
     def chain_copy(m, source, way, first):
@@ -123,24 +124,24 @@
 
     def plane_copy(m, source, to, origin, part=None):
         block = piece(m, source, core, partner(origin), part)
-        k, h = to ^ origin, 0 if part is None else part
-        return remote(block, block, plane_send.at[m, source, k, h], plane_recv.at[m, source, k, h], partner(to), mat)
-
-    def plane_arrival(m, source, e, part=None):
-        block = piece(m, source, core, partner(e), part)
-        h = 0 if part is None else part
-        return remote(block, block, plane_send.at[m, source, e, h], plane_recv.at[m, source, e, h], partner(e), mat)
-
-    def core_copy(m, source, e, mine=True):
-        block = piece(m, source, core if mine else flip(core, 1, CORES), partner(e))
-        return remote(block, block, core_send.at[m, source, e], core_recv.at[m, source, e], pair, sibling)
+        k = to ^ origin
+        return remote(block, block, plane_send.at[m], plane_recv.at[m, source, k], partner(to), mat)
+
+    def plane_arrival(m, source, e):
+        block = piece(m, source, core, partner(e))
+        return remote(block, block, plane_send.at[m], plane_recv.at[m, source, e], partner(e), mat)
+
+    def core_copy(m, source, e):
+        block = piece(m, source, core, partner(e))
+        return remote(block, block, core_send.at[m], core_recv.at[m], pair, sibling)
 
     def core_whole(m):
-        if m == RIGHT:
+        if m is not LEFT:
             src, dst = r_hbm, r_ref.at[pl.ds(pl.multiple_of(mat * rows, rows), rows), :]
         else:
             src = dst = lt_ref.at[line, :, pl.ds(pl.multiple_of(core * rows, rows), rows)]
-        return remote(src, dst, core_send.at[m, line, 0], core_recv.at[m, line, 0], pair, sibling)
+        k = 1 if m is LEFT else 0
+        return remote(src, dst, whole_send.at[k], whole_recv.at[k], pair, sibling)
 
     def reaches(way, h):
         if way == UP:
@@ -152,20 +153,25 @@
             cond, source = reaches(way, h)
             act(way, cond, source)
 
-    def hop(m, h):
-        def act(way, cond, source):
+    def chain(make, cond):
+        chained.append((make, cond))
+        launch(make, cond)
+
+    def hop(m, h, ways=(UP, DOWN)):
+        for way in ways:
+            cond, source = reaches(way, h)
             pl.when(cond)(lambda: line_arrival(m, source).wait_recv())
             if h + 1 < nline:
                 more = line < nline - 1 if way == UP else line > 0
-                launch(lambda: chain_copy(m, source, way, False), cond & more)
-        both(h, act)
+                chain(lambda m=m, source=source, way=way: chain_copy(m, source, way, False), cond & more)
+
+    def spread_way(m, way, cond, source):
+        for e in straight:
+            launch(lambda e=e: plane_copy(m, source, e, 0), cond)
+        launch(lambda: core_copy(m, source, 0), cond)
 
     def spread_first(m, h):
-        def act(way, cond, source):
-            for e in straight:
-                launch(lambda e=e: plane_copy(m, source, e, 0), cond)
-            launch(lambda: core_copy(m, source, 0), cond)
-        both(h, act)
+        both(h, lambda way, cond, source: spread_way(m, way, cond, source))
 
     def spread_second(m, h):
         def act(way, cond, source):
@@ -180,33 +186,30 @@
     def spread_third(m, h):
         def act(way, cond, source):
             for e in far:
-                for part in range(2):
-                    pl.when(cond)(lambda e=e, part=part: plane_arrival(m, source, e, part).wait_recv())
+                pl.when(cond)(lambda e=e: plane_arrival(m, source, e).wait_recv())
                 launch(lambda e=e: core_copy(m, source, e), cond)
         both(h, act)
 
-    def spread_last(m, h):
-        def act(way, cond, source):
-            for e in range(npair):
-                pl.when(cond)(lambda e=e: core_copy(m, source, e, False).wait_recv())
-        both(h, act)
-
-    def depart(m):
-        launch(lambda: chain_copy(m, line, UP, True), line < nline - 1)
-        launch(lambda: chain_copy(m, line, DOWN, True), line > 0)
-        launch(lambda: core_whole(m))
+    def gathered(m):
+        if m is not LEFT:
+            return r_ref.at[pl.ds(0, (nline - 1) * rows), pl.ds(0, cols // 2)]
+        return lt_ref.at[pl.ds(0, nline - 1), :, pl.ds(0, rows)]
+
+    def spread_last(m):
+        await_bytes(gathered(m), core_recv.at[m])
+
+    def depart(m, way):
+        chain(lambda: chain_copy(m, line, way, True), line < nline - 1 if way == UP else line > 0)
 
     def early_source(position):
         return a_hbm.at[:, position, pl.ds(0, early), :]
 
     def early_copy(e):
-        return remote(early_source(partner(e)), early_ref.at[pair], first_send.at[e], first_recv.at[e],
+        return remote(early_source(partner(e)), early_ref.at[pair], first_send.at[0], first_recv.at[0],
                       partner(e), mat)
 
     def early_mix():
-        for e in peers:
-            early_copy(e).wait_recv()
-        early_local.wait()
+        await_bytes(early_ref, first_recv.at[0])
         load_a.wait()
         span = min(512, cols)
 
@@ -221,12 +224,14 @@
 
         lax.fori_loop(0, cols // span, columns, 0)
 
-    depart(RIGHT)
+    for turn_of in range(2):
+        depart(turn_of, UP)
+        depart(1 - turn_of, DOWN)
+    launch(lambda: core_whole(0))
     if early:
         for e in peers[::-1]:
             launch(lambda e=e: early_copy(e))
-        early_local = pltpu.make_async_copy(early_source(pair), early_ref.at[pair], first_recv.at[0])
-        early_local.start()
+        pltpu.make_async_copy(early_source(pair), early_ref.at[pair], first_recv.at[0]).start()
 
     load_l.wait()
     lanes = pl.ds(pl.multiple_of(core * rows, rows), rows)
@@ -258,34 +263,43 @@
             == lax.broadcasted_iota(jnp.int32, full.shape, 1) % BLOCK)
     kron_ref[...] = jnp.where(same, full, 0.0).astype(jnp.bfloat16)
 
-    def right(stage, h):
-        if 1 <= h < nline:
-            if stage is spread_first:
-                hop(RIGHT, h)
-            stage(RIGHT, h)
-
-    for h in range(1, nline + 2):
-        right(spread_first, h)
-        if h == 2:
-            depart(LEFT)
-        if h == 2 and early:
-            early_mix()
-        if 1 <= h - 2 < nline - 1:
-            hop(LEFT, h - 2)
-        right(spread_second, h - 1)
-        if h == nline:
-            for k in range(1, nline - 1):
-                spread_first(LEFT, k)
-        right(spread_third, h - 2)
+    near = line // (nline // 2)
+    away = 1 - near
+
+    def hop_right(h):
+        for turn_of in range(2):
+            for way, m in ((UP, turn_of), (DOWN, 1 - turn_of)):
+                hop(m, h, (way,))
+                cond, source = reaches(way, h)
+                spread_way(m, way, cond & (away == m), source)
+
+    for h in hops:
+        hop_right(h)
+        if h == max(1, nline - 2):
+            depart(LEFT, UP)
+            depart(LEFT, DOWN)
+            launch(lambda: core_whole(LEFT))
+            if early:
+                early_mix()
+        if h > 1:
+            spread_second(away, h - 1)
+        if h == nline - 1 and nline > 2:
+            hop(LEFT, 1)
+    spread_second(away, nline - 1)
+    for h in hops:
+        spread_first(near, h)
+    for h in hops:
+        spread_third(away, h)
     load_r.wait()
     if not early:
         load_a.wait()
-    core_whole(RIGHT).wait_recv()
-    for h in hops:
-        spread_last(RIGHT, h)
+    for h in range(2, nline - 1):
+        hop(LEFT, h)
+    core_whole(0).wait_recv()
+    spread_last(away)
 
     def swap_copy(s, i, f):
-        return remote(h_ref.at[s], g_ref.at[s], swap_send.at[s], swap_recv.at[s], pair, place(i, f))
+        return remote(h_ref.at[s], g_ref.at[s], swap_send.at[0], swap_recv.at[s], pair, place(i, f))
 
     def half(i, f):
         start = pl.multiple_of(place(i, f) * width, width)
@@ -303,10 +317,10 @@
         return g_ref.at[s, :, position, pl.ds(early, late), :]
 
     def in_copy(s, e):
-        return remote(in_rows(s, partner(e)), x_ref.at[s, pair], in_send.at[s, e], in_recv.at[s, e], partner(e), mat)
+        return remote(in_rows(s, partner(e)), x_ref.at[s, pair], in_send.at[0], in_recv.at[s], partner(e), mat)
 
     def in_local(s):
-        return pltpu.make_async_copy(in_rows(s, pair), x_ref.at[s, pair], in_recv.at[s, 0])
+        return pltpu.make_async_copy(in_rows(s, pair), x_ref.at[s, pair], in_recv.at[s])
 
     def out_rows(s, start, count):
         at = flip(core, s % CORES, CORES) * rows + pair * strip + start
@@ -314,18 +328,18 @@
 
     def pass_copy(s, e):
         return remote(g_ref.at[s, :, partner(e), pl.ds(0, early), :], out_rows(s, 0, early),
-                      pass_send.at[s, e], pass_recv.at[s, e], partner(e), mat)
+                      pass_send.at[0], out_recv.at[s], partner(e), mat)
 
     def pass_local(s):
         return pltpu.make_async_copy(g_ref.at[s, :, pair, pl.ds(0, early), :], out_rows(s, 0, early),
-                                     pass_recv.at[s, 0])
+                                     out_recv.at[s])
 
     def out_copy(s, e):
-        return remote(y_ref.at[s, partner(e)], out_rows(s, early, late), out_send.at[s, e], out_recv.at[s, e],
+        return remote(y_ref.at[s, partner(e)], out_rows(s, early, late), out_send.at[0], out_recv.at[s],
                       partner(e), mat)
 
     def out_local(s):
-        return pltpu.make_async_copy(y_ref.at[s, pair], out_rows(s, early, late), out_recv.at[s, 0])
+        return pltpu.make_async_copy(y_ref.at[s, pair], out_rows(s, early, late), out_recv.at[s])
 
     def enter(s):
         if s > 0:
@@ -339,9 +353,7 @@
             pass_local(s).start()
 
     def mix(s):
-        for e in peers:
-            in_copy(s, e).wait_recv()
-        in_local(s).wait()
+        await_bytes(x_ref.at[s], in_recv.at[s])
 
         def chunk(b, carry):
             at = pl.ds(pl.multiple_of(b * BLOCK, BLOCK), BLOCK)
@@ -358,13 +370,7 @@
     tile = min(512, cols)
 
     def arrived(s):
-        for e in peers:
-            out_copy(s, e).wait_recv()
-        out_local(s).wait()
-        if early:
-            for e in peers:
-                pass_copy(s, e).wait_recv()
-            pass_local(s).wait()
+        await_bytes(z_ref.at[s // CORES, :, pl.ds(0, rows), :], out_recv.at[s])
 
     steps = cols // tile
 
@@ -401,14 +407,18 @@
                 lax.fori_loop(0, ntg * steps, product(i, f, i + f > 0, False), 0)
         for t in range(ntg):
             lax.fori_loop(t * steps, (t + 1) * steps, product(i, CORES - 1, True, True), 0)
-            pltpu.make_async_copy(stage_ref.at[t], out_hbm.at[t], store_sem.at[t]).start()
 
     lax.fori_loop(CORES, 2 * CORES, rotate, 0)
+    for h in hops:
+        spread_second(near, h)
+    for h in range(1, nline - 1):
+        spread_first(LEFT, h)
+    for h in hops:
+        spread_third(near, h)
+    spread_last(near)
     g_ref[0] = half(0, 0)
     enter(0)
     lax.fori_loop(1, CORES, rotate, 0)
-    hop(LEFT, nline - 1)
-    spread_first(LEFT, nline - 1)
     enter(1)
     lax.fori_loop(2 * CORES, nmat, rotate, 0)
 
@@ -419,26 +429,44 @@
                 enter(first + f)
         for f in range(CORES):
             mix(first + f)
-            if i == 0:
-                for h in hops:
-                    (spread_second if f == 0 else spread_third)(LEFT, h)
-        if i == 1:
-            core_whole(LEFT).wait_recv()
-            for h in hops:
-                spread_last(LEFT, h)
-        if i > 0:
-            finish(i - 1)
+            stage = i * CORES + f
+            last = nline - 1
+            if stage == 0:
+                for h in range(1, last):
+                    spread_second(LEFT, h)
+                hop(LEFT, last)
+                spread_first(LEFT, last)
+            if stage == 1:
+                for h in range(1, last):
+                    spread_third(LEFT, h)
+            if stage == 2:
+                spread_second(LEFT, last)
+            if stage == min(4, nmat - 1):
+                spread_third(LEFT, last)
+            if i > 0 and f == 0:
+                if i == 1:
+                    core_whole(LEFT).wait_recv()
+                if i == min(2, nline - 1):
+                    spread_last(LEFT)
+                finish(i - 1)
     finish_last()
 
-    for s in range(1, nmat):
-        swap_copy(s, s // CORES, s % CORES).wait_send()
-    for make, cond in sent:
-        if cond is None:
-            make().wait_send()
-        else:
-            pl.when(cond)(lambda make=make: make().wait_send())
-    for t in range(ntg):
-        pltpu.make_async_copy(stage_ref.at[t], out_hbm.at[t], store_sem.at[t]).wait()
+    count = (nline - 1) * (npair - 1)
+    for m in range(2):
+        await_bytes(r_ref.at[pl.ds(0, count * strip), pl.ds(0, cols // 2)], plane_send.at[m])
+    await_bytes(lt_ref.at[pl.ds(0, nline - 1), pl.ds(0, (npair - 1) * mpiece), pl.ds(0, rows)], plane_send.at[LEFT])
+    for m in range(LEFT + 1):
+        await_bytes(gathered(m), core_send.at[m])
+    for m in (0, LEFT):
+        core_whole(m).wait_send()
+    await_bytes(h_ref.at[pl.ds(1, nmat - 1)], swap_send.at[0])
+    await_bytes(x_ref.at[:, pl.ds(0, npair - 1)], in_send.at[0])
+    await_bytes(y_ref.at[:, pl.ds(0, npair - 1)], out_send.at[0])
+    if early:
+        await_bytes(early_ref.at[pl.ds(0, npair - 1)], first_send.at[0])
+        await_bytes(g_ref.at[:, :, pl.ds(0, npair - 1), pl.ds(0, early), :], pass_send.at[0])
+    for make, cond in chained:
+        pl.when(cond)(lambda make=make: make().wait_send())
 
 
 def shards(operators, left_rot, right_rot, integrals, pair_index, target_index):
@@ -456,9 +484,9 @@
     scalars = pl.BlockSpec(memory_space=pltpu.SMEM)
     return pl.pallas_call(
         functools.partial(kernel, npair, nline),
-        out_shape=jax.ShapeDtypeStruct((ntg, cols, width), bf16),
+        out_shape=pltpu.VMEM((ntg, cols, width), bf16),
         in_specs=[scalars, scalars, anywhere, anywhere, anywhere, anywhere],
-        out_specs=anywhere,
+        out_specs=pl.BlockSpec(memory_space=pltpu.VMEM),
         scratch_shapes=[
             pltpu.VMEM((own, npair, strip, cols), bf16),
             pltpu.VMEM((npair, own, BLOCK, cols), bf16),
@@ -474,20 +502,17 @@
             pltpu.VMEM((nmat, npair, ntg, strip - early, width), bf16),
             pltpu.VMEM((nline, ntg, CORES * rows, width), bf16),
             pltpu.VMEM((ntg, cols, width), f32),
-            pltpu.VMEM((ntg, cols, width), bf16),
             dma((4,)),
-            dma((2, nline, 2)), dma((2, nline)),
-            dma((2, nline, npair, 2)), dma((2, nline, npair, 2)),
-            dma((2, nline, npair)), dma((2, nline, npair)),
-            dma((nmat,)), dma((nmat,)),
-            dma((npair,)), dma((npair,)),
-            dma((nmat, npair)), dma((nmat, npair)),
-            dma((nmat, npair)), dma((nmat, npair)),
-            dma((nmat, npair)), dma((nmat, npair)),
-            dma((ntg,)),
+            dma((3, nline, 2)), dma((3, nline)),
+            dma((3,)), dma((3, nline, npair)),
+            dma((3,)), dma((3,)), dma((2,)), dma((2,)),
+            dma((1,)), dma((nmat,)),
+            dma((1,)), dma((1,)),
+            dma((1,)), dma((nmat,)),
+            dma((1,)), dma((1,)), dma((nmat,)),
         ],
         compiler_params=pltpu.CompilerParams(
-            collective_id=0, has_side_effects=True, vmem_limit_bytes=67043328),
+            collective_id=0, has_side_effects=True, vmem_limit_bytes=56623104),
     )(target_index, pair_index, operators.reshape(own, npair, strip, cols), right_rot, left_rot, integrals)
 
 

time: 169 us -> 158 us (0.935)
  Pallas kernels: 165 us -> 156 us
  local copies, waits for them, and re-layouts: 4.47 us -> 2.02 us
    pallas_call x1, Pallas kernels: 165 us -> 156 us  [shards(): pl.pallas_call(functools.partial(kernel, npair, nline), out_shape=pltpu.V...]
    unnamed x1, local copies, waits for them, and re-layouts: 4.47 us -> 2.02 us
where the time goes in v4:
time: 158 us
  Pallas kernels  156 us (99%)
  local copies, waits for them, and re-layouts  2.02 us (1%)
    pallas_call x1, Pallas kernels, shards(): pl.pallas_call(functools.partial(kernel, npair, nline), out_shape=pltpu.V...  156 us

profile of v4, /device:TPU:0, one launch (start us, length us, event | category | flops | bytes accessed | tf_op | source)
XLA Modules:
  0.0 157.7 jit_solution(12502628412500411925)
XLA Ops:
  0.0 155.7 %shard_map.64 = bf16[4,2048,256]{2,1,0:T(8,128)(2,1)S(1)} custom-call(s32[16]{0:T(128)} %targets_ref.1, s32[16]{0:T(128)} %pairs_ref.1, bf16[4,4,64,2048]{3,2,1,0:T(8,128)(2,1)} %bitcast.1, bf16[256,2048]{1,0:T(8,128)(2,1)} %r_hbm.1, bf16[256,2048]{1,0:T(8,128)(2,1)} %l_hbm.1, f32[1024,1024]{1,0:T(8,128)} %integrals_hbm.1), custom_call_target="tpu_custom_call" | custom-call | tf_op jit(solution)/shard_map/pallas_call | solution.py:485
  155.7 2.0 %copy.8 = bf16[4,2048,256]{2,1,0:T(8,128)(2,1)} copy(bf16[4,2048,256]{2,1,0:T(8,128)(2,1)S(1)} %shard_map.64) | data formatting | bytes 8388608

commit v5 on v4

--- a/solution.py
+++ b/solution.py
@@ -10,6 +10,7 @@
 CORES = 2
 NEAR = 2
 BLOCK = 16
+BESIDE = 3
 LEFT = 2
 UP, DOWN = 0, 1
 MESH_ID = pl.DeviceIdType.MESH
@@ -38,6 +39,7 @@
            a_ref, early_ref, r_ref, l_ref, lt_ref, integrals_ref, rows_ref, kron_ref, h_ref, g_ref, x_ref, y_ref, z_ref,
            acc_ref,
            load_sem, line_send, line_recv, plane_send, plane_recv, core_send, core_recv, whole_send, whole_recv,
+           next_send, next_recv,
            swap_send, swap_recv, first_send, first_recv, in_send, in_recv, pass_send, out_send, out_recv):
     own, _, strip, cols = a_hbm.shape
     rows = npair * strip
@@ -131,9 +133,10 @@
         block = piece(m, source, core, partner(e))
         return remote(block, block, plane_send.at[m], plane_recv.at[m, source, e], partner(e), mat)
 
-    def core_copy(m, source, e):
+    def core_copy(m, source, e, group=None):
         block = piece(m, source, core, partner(e))
-        return remote(block, block, core_send.at[m], core_recv.at[m], pair, sibling)
+        k = m if group is None else group
+        return remote(block, block, core_send.at[k], core_recv.at[k], pair, sibling)
 
     def core_whole(m):
         if m is not LEFT:
@@ -165,6 +168,14 @@
                 more = line < nline - 1 if way == UP else line > 0
                 chain(lambda m=m, source=source, way=way: chain_copy(m, source, way, False), cond & more)
 
+    def left_hop(h):
+        if h + 1 < nline:
+            for way in (UP, DOWN):
+                cond, source = reaches(way, h)
+                more = cond & (line < nline - 1 if way == UP else line > 0)
+                pl.when(more)(lambda: line_arrival(LEFT, source).wait_recv())
+                chain(lambda source=source, way=way: chain_copy(LEFT, source, way, False), more)
+
     def spread_way(m, way, cond, source):
         for e in straight:
             launch(lambda e=e: plane_copy(m, source, e, 0), cond)
@@ -173,8 +184,33 @@
     def spread_first(m, h):
         both(h, lambda way, cond, source: spread_way(m, way, cond, source))
 
+    beside = flip(line, 1, nline)
+
+    def next_copy(e):
+        block = piece(LEFT, line, core, partner(e))
+        return remote(block, block, next_send.at[0], next_recv.at[0], pair, beside * CORES + core)
+
+    def left_first(h):
+        def act(way, cond, source):
+            ends = cond if h + 1 == nline else cond & (line == (nline - 1 if way == UP else 0))
+            pl.when(ends)(lambda: line_arrival(LEFT, source).wait_recv())
+            if h == 1:
+                through = cond & (line % 2 == (0 if way == UP else 1))
+                launch(lambda: core_copy(LEFT, source, 0, BESIDE), cond & (line % 2 == (1 if way == UP else 0)))
+            else:
+                through = cond
+            spread_way(LEFT, way, through, source)
+        both(h, act)
+
+    def left_beside():
+        await_bytes(lt_ref.at[0, pl.ds(0, (npair - 1) * mpiece), pl.ds(0, rows)], next_recv.at[0])
+        for e in peers:
+            launch(lambda e=e: core_copy(LEFT, beside, e, BESIDE))
+
     def spread_second(m, h):
         def act(way, cond, source):
+            if m is LEFT and h == 1:
+                cond = cond & (line % 2 == (0 if way == UP else 1))
             for e in straight:
                 pl.when(cond)(lambda e=e: plane_arrival(m, source, e).wait_recv())
                 for to in straight:
@@ -185,18 +221,23 @@
 
     def spread_third(m, h):
         def act(way, cond, source):
+            if m is LEFT and h == 1:
+                cond = cond & (line % 2 == (0 if way == UP else 1))
             for e in far:
                 pl.when(cond)(lambda e=e: plane_arrival(m, source, e).wait_recv())
                 launch(lambda e=e: core_copy(m, source, e), cond)
         both(h, act)
 
     def gathered(m):
-        if m is not LEFT:
-            return r_ref.at[pl.ds(0, (nline - 1) * rows), pl.ds(0, cols // 2)]
-        return lt_ref.at[pl.ds(0, nline - 1), :, pl.ds(0, rows)]
+        if m is BESIDE:
+            return lt_ref.at[0, :, pl.ds(0, rows)]
+        if m is LEFT:
+            return lt_ref.at[pl.ds(0, nline - 2), :, pl.ds(0, rows)]
+        return r_ref.at[pl.ds(0, (nline - 1) * rows), pl.ds(0, cols // 2)]
 
     def spread_last(m):
-        await_bytes(gathered(m), core_recv.at[m])
+        if m is not LEFT or nline > 2:
+            await_bytes(gathered(m), core_recv.at[m])
 
     def depart(m, way):
         chain(lambda: chain_copy(m, line, way, True), line < nline - 1 if way == UP else line > 0)
@@ -266,26 +307,26 @@
     near = line // (nline // 2)
     away = 1 - near
 
-    def hop_right(h):
-        for turn_of in range(2):
-            for way, m in ((UP, turn_of), (DOWN, 1 - turn_of)):
-                hop(m, h, (way,))
-                cond, source = reaches(way, h)
-                spread_way(m, way, cond & (away == m), source)
-
-    for h in hops:
-        hop_right(h)
-        if h == max(1, nline - 2):
-            depart(LEFT, UP)
-            depart(LEFT, DOWN)
-            launch(lambda: core_whole(LEFT))
-            if early:
-                early_mix()
-        if h > 1:
-            spread_second(away, h - 1)
-        if h == nline - 1 and nline > 2:
-            hop(LEFT, 1)
+    def hop_right(h, turn_of):
+        for way, m in ((UP, turn_of), (DOWN, 1 - turn_of)):
+            hop(m, h, (way,))
+            cond, source = reaches(way, h)
+            spread_way(m, way, cond & (away == m), source)
+
+    for h in range(1, nline - 1):
+        hop_right(h, 0)
+        hop_right(h, 1)
+    depart(LEFT, UP)
+    depart(LEFT, DOWN)
+    launch(lambda: core_whole(LEFT))
+    hop_right(nline - 1, 0)
+    if early:
+        early_mix()
+    for h in range(1, nline - 1):
+        spread_second(away, h)
+    left_hop(1)
     spread_second(away, nline - 1)
+    hop_right(nline - 1, 1)
     for h in hops:
         spread_first(near, h)
     for h in hops:
@@ -293,13 +334,13 @@
     load_r.wait()
     if not early:
         load_a.wait()
-    for h in range(2, nline - 1):
-        hop(LEFT, h)
     core_whole(0).wait_recv()
     spread_last(away)
 
-    def swap_copy(s, i, f):
-        return remote(h_ref.at[s], g_ref.at[s], swap_send.at[0], swap_recv.at[s], pair, place(i, f))
+    def swap_copy(s, i, f, e):
+        strips = partner(e)
+        return remote(h_ref.at[s, :, strips], g_ref.at[s, :, strips], swap_send.at[0], swap_recv.at[s, e],
+                      pair, place(i, f))
 
     def half(i, f):
         start = pl.multiple_of(place(i, f) * width, width)
@@ -310,7 +351,8 @@
     def rotate(s, carry):
         i, f = s // CORES, s % CORES
         h_ref[s] = half(i, f)
-        swap_copy(s, i, f).start()
+        for e in peers[::-1] + (0,):
+            swap_copy(s, i, f, e).start()
         return carry
 
     def in_rows(s, position):
@@ -342,10 +384,11 @@
         return pltpu.make_async_copy(y_ref.at[s, pair], out_rows(s, early, late), out_recv.at[s])
 
     def enter(s):
-        if s > 0:
-            swap_copy(s, s // CORES, s % CORES).wait_recv()
-        for e in peers[::-1]:
-            launch(lambda e=e: in_copy(s, e))
+        for e in peers[::-1] + (0,):
+            if s > 0:
+                swap_copy(s, s // CORES, s % CORES, e).wait_recv()
+            if e:
+                launch(lambda e=e: in_copy(s, e))
         in_local(s).start()
         if early:
             for e in peers[::-1]:
@@ -367,7 +410,7 @@
             launch(lambda e=e: out_copy(s, e))
         out_local(s).start()
 
-    tile = min(512, cols)
+    tile = cols
 
     def arrived(s):
         await_bytes(z_ref.at[s // CORES, :, pl.ds(0, rows), :], out_recv.at[s])
@@ -409,10 +452,12 @@
             lax.fori_loop(t * steps, (t + 1) * steps, product(i, CORES - 1, True, True), 0)
 
     lax.fori_loop(CORES, 2 * CORES, rotate, 0)
+    for h in range(2, nline - 1):
+        left_hop(h)
     for h in hops:
         spread_second(near, h)
     for h in range(1, nline - 1):
-        spread_first(LEFT, h)
+        left_first(h)
     for h in hops:
         spread_third(near, h)
     spread_last(near)
@@ -420,13 +465,18 @@
     enter(0)
     lax.fori_loop(1, CORES, rotate, 0)
     enter(1)
-    lax.fori_loop(2 * CORES, nmat, rotate, 0)
+    lax.fori_loop(2 * CORES, min(3 * CORES, nmat), rotate, 0)
+    for e in peers:
+        launch(lambda e=e: next_copy(e))
+    lax.fori_loop(min(3 * CORES, nmat), nmat, rotate, 0)
 
     for i in range(nline):
         first = i * CORES
         if i > 0:
             for f in range(CORES):
                 enter(first + f)
+        if i == min(3, nline - 1):
+            left_beside()
         for f in range(CORES):
             mix(first + f)
             stage = i * CORES + f
@@ -434,8 +484,7 @@
             if stage == 0:
                 for h in range(1, last):
                     spread_second(LEFT, h)
-                hop(LEFT, last)
-                spread_first(LEFT, last)
+                left_first(last)
             if stage == 1:
                 for h in range(1, last):
                     spread_third(LEFT, h)
@@ -443,19 +492,25 @@
                 spread_second(LEFT, last)
             if stage == min(4, nmat - 1):
                 spread_third(LEFT, last)
-            if i > 0 and f == 0:
+            if i > 0 and f == (CORES - 1 if i == nline - 1 else 0):
                 if i == 1:
                     core_whole(LEFT).wait_recv()
                 if i == min(2, nline - 1):
                     spread_last(LEFT)
+                if i == min(3, nline - 1):
+                    spread_last(BESIDE)
                 finish(i - 1)
     finish_last()
 
     count = (nline - 1) * (npair - 1)
     for m in range(2):
         await_bytes(r_ref.at[pl.ds(0, count * strip), pl.ds(0, cols // 2)], plane_send.at[m])
-    await_bytes(lt_ref.at[pl.ds(0, nline - 1), pl.ds(0, (npair - 1) * mpiece), pl.ds(0, rows)], plane_send.at[LEFT])
-    for m in range(LEFT + 1):
+    if nline > 2:
+        await_bytes(lt_ref.at[pl.ds(0, nline - 2), pl.ds(0, (npair - 1) * mpiece), pl.ds(0, rows)],
+                    plane_send.at[LEFT])
+        await_bytes(gathered(LEFT), core_send.at[LEFT])
+    await_bytes(lt_ref.at[0, pl.ds(0, (npair - 1) * mpiece), pl.ds(0, rows)], next_send.at[0])
+    for m in (0, 1, BESIDE):
         await_bytes(gathered(m), core_send.at[m])
     for m in (0, LEFT):
         core_whole(m).wait_send()
@@ -505,8 +560,9 @@
             dma((4,)),
             dma((3, nline, 2)), dma((3, nline)),
             dma((3,)), dma((3, nline, npair)),
-            dma((3,)), dma((3,)), dma((2,)), dma((2,)),
-            dma((1,)), dma((nmat,)),
+            dma((4,)), dma((4,)), dma((2,)), dma((2,)),
+            dma((1,)), dma((1,)),
+            dma((1,)), dma((nmat, npair)),
             dma((1,)), dma((1,)),
             dma((1,)), dma((nmat,)),
             dma((1,)), dma((1,)), dma((nmat,)),

time: 158 us -> 147 us (0.930)
  Pallas kernels: 156 us -> 145 us
    pallas_call x1, Pallas kernels: 156 us -> 145 us  [shards(): pl.pallas_call(functools.partial(kernel, npair, nline), out_shape=pltpu.V...]
where the time goes in v5:
time: 147 us
  Pallas kernels  145 us (99%)
  local copies, waits for them, and re-layouts  2.02 us (1%)
    pallas_call x1, Pallas kernels, shards(): pl.pallas_call(functools.partial(kernel, npair, nline), out_shape=pltpu.V...  145 us

profile of v5, /device:TPU:0, one launch (start us, length us, event | category | flops | bytes accessed | tf_op | source)
XLA Modules:
  0.0 146.5 jit_solution(14112702131581384719)
XLA Ops:
  0.0 144.5 %shard_map.64 = bf16[4,2048,256]{2,1,0:T(8,128)(2,1)S(1)} custom-call(s32[16]{0:T(128)} %targets_ref.1, s32[16]{0:T(128)} %pairs_ref.1, bf16[4,4,64,2048]{3,2,1,0:T(8,128)(2,1)} %bitcast.1, bf16[256,2048]{1,0:T(8,128)(2,1)} %r_hbm.1, bf16[256,2048]{1,0:T(8,128)(2,1)} %l_hbm.1, f32[1024,1024]{1,0:T(8,128)} %integrals_hbm.1), custom_call_target="tpu_custom_call" | custom-call | tf_op jit(solution)/shard_map/pallas_call | solution.py:540
  144.5 2.0 %copy.8 = bf16[4,2048,256]{2,1,0:T(8,128)(2,1)} copy(bf16[4,2048,256]{2,1,0:T(8,128)(2,1)S(1)} %shard_map.64) | data formatting | bytes 8388608

commit v6 on v5

--- a/solution.py
+++ b/solution.py
@@ -24,11 +24,17 @@
     return total
 
 
-def offset_of(i, nline):
-    if isinstance(i, int):
-        return 0 if i == 0 else (nline - 1 - (i - 1) // 2 if i % 2 == 1 else i // 2)
-    odd = i % 2
-    return odd * (nline - 1 - (i - 1) // 2) + (1 - odd) * (i // 2)
+def offset_of(i, line, nline):
+    if nline == 4 and i % 2 == 1:
+        inner = (line + 1) // 2 % 2
+        return 3 - inner if i == 1 else 2 + inner
+    return 0 if i == 0 else (nline - 1 - (i - 1) // 2 if i % 2 == 1 else i // 2)
+
+
+def order_of(d, line, nline):
+    if nline == 4 and d >= 2:
+        return 1 + 2 * ((line + 1) // 2 % 2)
+    return next(i for i in range(nline) if offset_of(i, 0, nline) == d)
 
 
 def early_rows(own, ntg, strip):
@@ -58,7 +64,7 @@
     hops = range(1, nline)
 
     def place(i, f):
-        return flip(line, offset_of(i, nline), nline) * CORES + flip(core, f, CORES)
+        return flip(line, offset_of(i, line, nline), nline) * CORES + flip(core, f, CORES)
 
     def partner(e):
         return flip(pair, e, npair)
@@ -89,12 +95,17 @@
         copy.start()
 
     barrier = pltpu.get_barrier_semaphore()
-    for s in range(1, nmat):
-        pl.semaphore_signal(barrier, inc=1, device_id={"pair": pair, "mat": place(s // CORES, s % CORES)},
-                            device_id_type=MESH_ID)
+
+    def greet(pair_id, mat_id):
+        pl.semaphore_signal(barrier, inc=1, device_id={"pair": pair_id, "mat": mat_id}, device_id_type=MESH_ID)
+
     for e in peers:
-        pl.semaphore_signal(barrier, inc=1, device_id={"pair": partner(e), "mat": mat}, device_id_type=MESH_ID)
-    pl.semaphore_wait(barrier, nmat - 1 + len(peers))
+        greet(partner(e), mat)
+    greet(pair, sibling)
+    pl.when(line > 0)(lambda: greet(pair, mat - CORES))
+    pl.when(line < nline - 1)(lambda: greet(pair, mat + CORES))
+    above, below = 1 - (line + 1) // nline, (line + nline - 1) // nline
+    pl.semaphore_wait(barrier, len(peers) + 1 + above + below)
 
     def piece(m, source, c, origin, part=None):
         if m is not LEFT:
@@ -337,23 +348,32 @@
     core_whole(0).wait_recv()
     spread_last(away)
 
-    def swap_copy(s, i, f, e):
+    def swap_copy(d, f, e):
         strips = partner(e)
-        return remote(h_ref.at[s, :, strips], g_ref.at[s, :, strips], swap_send.at[0], swap_recv.at[s, e],
-                      pair, place(i, f))
-
-    def half(i, f):
-        start = pl.multiple_of(place(i, f) * width, width)
+        slot = order_of(d, line, nline) * CORES + f
+        there = flip(line, d, nline) * CORES + flip(core, f, CORES)
+        return remote(h_ref.at[d * CORES + f, :, strips], g_ref.at[slot, :, strips], swap_send.at[0],
+                      swap_recv.at[slot, e], pair, there)
+
+    def swap_arrival(s, e):
+        block = g_ref.at[s, :, partner(e)]
+        return remote(block, block, swap_send.at[0], swap_recv.at[s, e], pair, sibling)
+
+    def half(d, f):
+        there = flip(line, d, nline) * CORES + flip(core, f, CORES)
+        start = pl.multiple_of(there * width, width)
         block = jnp.dot(a_ref[...].reshape(own * rows, cols), r_ref[:, pl.ds(start, width)],
                         preferred_element_type=jnp.float32)
         return block.astype(jnp.bfloat16).reshape(own, npair, strip, width)
 
-    def rotate(s, carry):
-        i, f = s // CORES, s % CORES
-        h_ref[s] = half(i, f)
-        for e in peers[::-1] + (0,):
-            swap_copy(s, i, f, e).start()
-        return carry
+    def rotate(d, first=0):
+        def one(f, carry):
+            h_ref[d * CORES + f] = half(d, f)
+            for e in peers[::-1] + (0,):
+                swap_copy(d, f, e).start()
+            return carry
+
+        lax.fori_loop(first, CORES, one, 0)
 
     def in_rows(s, position):
         return g_ref.at[s, :, position, pl.ds(early, late), :]
@@ -386,7 +406,7 @@
     def enter(s):
         for e in peers[::-1] + (0,):
             if s > 0:
-                swap_copy(s, s // CORES, s % CORES, e).wait_recv()
+                swap_arrival(s, e).wait_recv()
             if e:
                 launch(lambda e=e: in_copy(s, e))
         in_local(s).start()
@@ -418,7 +438,7 @@
     steps = cols // tile
 
     def product(i, f, add, last):
-        source = flip(line, offset_of(i, nline), nline)
+        source = flip(line, offset_of(i, line, nline), nline)
         if f is None:
             depth = pl.ds(0, CORES * rows)
         else:
@@ -451,7 +471,8 @@
         for t in range(ntg):
             lax.fori_loop(t * steps, (t + 1) * steps, product(i, CORES - 1, True, True), 0)
 
-    lax.fori_loop(CORES, 2 * CORES, rotate, 0)
+    for d in range(nline - 1, nline // 2 - 1, -1):
+        rotate(d)
     for h in range(2, nline - 1):
         left_hop(h)
     for h in hops:
@@ -463,12 +484,12 @@
     spread_last(near)
     g_ref[0] = half(0, 0)
     enter(0)
-    lax.fori_loop(1, CORES, rotate, 0)
+    rotate(0, 1)
     enter(1)
-    lax.fori_loop(2 * CORES, min(3 * CORES, nmat), rotate, 0)
+    for d in range(1, nline // 2):
+        rotate(d)
     for e in peers:
         launch(lambda e=e: next_copy(e))
-    lax.fori_loop(min(3 * CORES, nmat), nmat, rotate, 0)
 
     for i in range(nline):
         first = i * CORES

time: 147 us -> 145 us (0.986)
  Pallas kernels: 145 us -> 143 us
    pallas_call x1, Pallas kernels: 145 us -> 143 us  [shards(): pl.pallas_call(functools.partial(kernel, npair, nline), out_shape=pltpu.V...]
where the time goes in v6:
time: 145 us
  Pallas kernels  143 us (99%)
  local copies, waits for them, and re-layouts  2.02 us (1%)
    pallas_call x1, Pallas kernels, shards(): pl.pallas_call(functools.partial(kernel, npair, nline), out_shape=pltpu.V...  143 us

profile of v6, /device:TPU:0, one launch (start us, length us, event | category | flops | bytes accessed | tf_op | source)
XLA Modules:
  0.0 144.9 jit_solution(8258092595145844337)
XLA Ops:
  0.0 142.9 %shard_map.64 = bf16[4,2048,256]{2,1,0:T(8,128)(2,1)S(1)} custom-call(s32[16]{0:T(128)} %targets_ref.1, s32[16]{0:T(128)} %pairs_ref.1, bf16[4,4,64,2048]{3,2,1,0:T(8,128)(2,1)} %bitcast.1, bf16[256,2048]{1,0:T(8,128)(2,1)} %r_hbm.1, bf16[256,2048]{1,0:T(8,128)(2,1)} %l_hbm.1, f32[1024,1024]{1,0:T(8,128)} %integrals_hbm.1), custom_call_target="tpu_custom_call" | custom-call | tf_op jit(solution)/shard_map/pallas_call | solution.py:561
  142.9 2.0 %copy.8 = bf16[4,2048,256]{2,1,0:T(8,128)(2,1)} copy(bf16[4,2048,256]{2,1,0:T(8,128)(2,1)S(1)} %shard_map.64) | data formatting | bytes 8388608

commit v7 on v6

--- a/solution.py
+++ b/solution.py
@@ -41,15 +41,15 @@
     return BLOCK if own == ntg and strip > BLOCK else 0
 
 
-def kernel(npair, nline, targets_ref, pairs_ref, a_hbm, r_hbm, l_hbm, integrals_hbm, stage_ref,
-           a_ref, early_ref, r_ref, l_ref, lt_ref, integrals_ref, rows_ref, kron_ref, h_ref, g_ref, x_ref, y_ref, z_ref,
+def kernel(npair, nline, targets_hbm, pairs_hbm, a_hbm, r_hbm, l_hbm, integrals_hbm, stage_ref,
+           targets_ref, pairs_ref, a_ref, early_ref, r_ref, l_ref, lt_ref, integrals_ref, rows_ref, kron_ref, h_ref, g_ref, x_ref, y_ref, z_ref,
            acc_ref,
            load_sem, line_send, line_recv, plane_send, plane_recv, core_send, core_recv, whole_send, whole_recv,
            next_send, next_recv,
            swap_send, swap_recv, first_send, first_recv, in_send, in_recv, pass_send, out_send, out_recv):
     own, _, strip, cols = a_hbm.shape
     rows = npair * strip
-    ntgt, nsel = targets_ref.shape[0], pairs_ref.shape[0]
+    ntgt, nsel = targets_hbm.shape[0], pairs_hbm.shape[0]
     ntg = ntgt // npair
     nmat = nline * CORES
     width = cols // nmat
@@ -70,6 +70,7 @@
         return flip(pair, e, npair)
 
     sibling = line * CORES + flip(core, 1, CORES)
+    at_end = (line == 0) | (line == nline - 1)
 
     def remote(src, dst, send, recv, pair_id, mat_id):
         return pltpu.make_async_remote_copy(
@@ -85,13 +86,14 @@
     def await_bytes(block, sem):
         pltpu.make_async_copy(block, block, sem).wait()
 
-    chained = []
 
     load_r = pltpu.make_async_copy(r_hbm, r_ref.at[pl.ds(pl.multiple_of(mat * rows, rows), rows), :], load_sem.at[0])
     load_l = pltpu.make_async_copy(l_hbm, l_ref, load_sem.at[1])
     load_i = pltpu.make_async_copy(integrals_hbm, integrals_ref, load_sem.at[2])
     load_a = pltpu.make_async_copy(a_hbm, a_ref, load_sem.at[3])
-    for copy in (load_l, load_i, load_r, load_a):
+    load_t = pltpu.make_async_copy(targets_hbm, targets_ref, load_sem.at[4])
+    load_p = pltpu.make_async_copy(pairs_hbm, pairs_ref, load_sem.at[5])
+    for copy in (load_t, load_p, load_l, load_i, load_r, load_a):
         copy.start()
 
     barrier = pltpu.get_barrier_semaphore()
@@ -128,21 +130,21 @@
     def chain_copy(m, source, way, first):
         block = piece(m, source, core, pair)
         step = 1 if way == UP else -1
-        return remote(own_piece(m) if first else block, block, line_send.at[m, source, way], line_recv.at[m, source],
+        return remote(own_piece(m) if first else block, block, line_send.at[m], line_recv.at[m, source],
                       pair, (line + step) * CORES + core)
 
     def line_arrival(m, source):
         block = piece(m, source, core, pair)
-        return remote(block, block, line_send.at[m, source, UP], line_recv.at[m, source], pair, sibling)
+        return remote(block, block, line_send.at[m], line_recv.at[m, source], pair, sibling)
 
     def plane_copy(m, source, to, origin, part=None):
         block = piece(m, source, core, partner(origin), part)
         k = to ^ origin
-        return remote(block, block, plane_send.at[m], plane_recv.at[m, source, k], partner(to), mat)
+        return remote(block, block, plane_send.at[m], plane_recv.at[m, source, k - 1], partner(to), mat)
 
     def plane_arrival(m, source, e):
         block = piece(m, source, core, partner(e))
-        return remote(block, block, plane_send.at[m], plane_recv.at[m, source, e], partner(e), mat)
+        return remote(block, block, plane_send.at[m], plane_recv.at[m, source, e - 1], partner(e), mat)
 
     def core_copy(m, source, e, group=None):
         block = piece(m, source, core, partner(e))
@@ -167,17 +169,13 @@
             cond, source = reaches(way, h)
             act(way, cond, source)
 
-    def chain(make, cond):
-        chained.append((make, cond))
-        launch(make, cond)
-
     def hop(m, h, ways=(UP, DOWN)):
         for way in ways:
             cond, source = reaches(way, h)
             pl.when(cond)(lambda: line_arrival(m, source).wait_recv())
             if h + 1 < nline:
                 more = line < nline - 1 if way == UP else line > 0
-                chain(lambda m=m, source=source, way=way: chain_copy(m, source, way, False), cond & more)
+                launch(lambda m=m, source=source, way=way: chain_copy(m, source, way, False), cond & more)
 
     def left_hop(h):
         if h + 1 < nline:
@@ -185,7 +183,7 @@
                 cond, source = reaches(way, h)
                 more = cond & (line < nline - 1 if way == UP else line > 0)
                 pl.when(more)(lambda: line_arrival(LEFT, source).wait_recv())
-                chain(lambda source=source, way=way: chain_copy(LEFT, source, way, False), more)
+                launch(lambda source=source, way=way: chain_copy(LEFT, source, way, False), more)
 
     def spread_way(m, way, cond, source):
         for e in straight:
@@ -251,7 +249,7 @@
             await_bytes(gathered(m), core_recv.at[m])
 
     def depart(m, way):
-        chain(lambda: chain_copy(m, line, way, True), line < nline - 1 if way == UP else line > 0)
+        launch(lambda: chain_copy(m, line, way, True), line < nline - 1 if way == UP else line > 0)
 
     def early_source(position):
         return a_hbm.at[:, position, pl.ds(0, early), :]
@@ -296,6 +294,8 @@
     lax.fori_loop(0, cols // 256, turn, 0)
 
     load_i.wait()
+    load_t.wait()
+    load_p.wait()
     for t in range(ntgt):
         rows_ref[pl.ds(t, 1), :] = integrals_ref[pl.ds(targets_ref[t], 1), :]
     picked = rows_ref[...]
@@ -541,8 +541,11 @@
     if early:
         await_bytes(early_ref.at[pl.ds(0, npair - 1)], first_send.at[0])
         await_bytes(g_ref.at[:, :, pl.ds(0, npair - 1), pl.ds(0, early), :], pass_send.at[0])
-    for make, cond in chained:
-        pl.when(cond)(lambda make=make: make().wait_send())
+    for m in range(LEFT + 1):
+        lanes = pl.ds(0, cols if m is LEFT else cols // 2)
+        pl.when(at_end)(lambda m=m, lanes=lanes: await_bytes(r_ref.at[pl.ds(0, strip), lanes], line_send.at[m]))
+        pl.when(jnp.logical_not(at_end))(
+            lambda m=m, lanes=lanes: await_bytes(r_ref.at[pl.ds(0, (nline + 1) * strip), lanes], line_send.at[m]))
 
 
 def shards(operators, left_rot, right_rot, integrals, pair_index, target_index):
@@ -557,13 +560,14 @@
     bf16, f32 = jnp.bfloat16, jnp.float32
     dma = pltpu.SemaphoreType.DMA
     anywhere = pl.BlockSpec(memory_space=pl.ANY)
-    scalars = pl.BlockSpec(memory_space=pltpu.SMEM)
     return pl.pallas_call(
         functools.partial(kernel, npair, nline),
         out_shape=pltpu.VMEM((ntg, cols, width), bf16),
-        in_specs=[scalars, scalars, anywhere, anywhere, anywhere, anywhere],
+        in_specs=[anywhere, anywhere, anywhere, anywhere, anywhere, anywhere],
         out_specs=pl.BlockSpec(memory_space=pltpu.VMEM),
         scratch_shapes=[
+            pltpu.SMEM((ntgt,), jnp.int32),
+            pltpu.SMEM((nsel,), jnp.int32),
             pltpu.VMEM((own, npair, strip, cols), bf16),
             pltpu.VMEM((npair, own, BLOCK, cols), bf16),
             pltpu.VMEM((cols, cols), bf16),
@@ -578,9 +582,9 @@
             pltpu.VMEM((nmat, npair, ntg, strip - early, width), bf16),
             pltpu.VMEM((nline, ntg, CORES * rows, width), bf16),
             pltpu.VMEM((ntg, cols, width), f32),
-            dma((4,)),
-            dma((3, nline, 2)), dma((3, nline)),
-            dma((3,)), dma((3, nline, npair)),
+            dma((6,)),
+            dma((3,)), dma((3, nline)),
+            dma((3,)), dma((3, nline, npair - 1)),
             dma((4,)), dma((4,)), dma((2,)), dma((2,)),
             dma((1,)), dma((1,)),
             dma((1,)), dma((nmat, npair)),

time: 145 us -> 144 us (level)
  no operation moved by 1% of the time
where the time goes in v7:
time: 144 us
  Pallas kernels  142 us (99%)
  local copies, waits for them, and re-layouts  2.02 us (1%)
    pallas_call x1, Pallas kernels, shards(): pl.pallas_call(functools.partial(kernel, npair, nline), out_shape=pltpu.V...  142 us

profile of v7, /device:TPU:0, one launch (start us, length us, event | category | flops | bytes accessed | tf_op | source)
XLA Modules:
  0.0 143.9 jit_solution(10605693067661180465)
XLA Ops:
  0.0 141.9 %shard_map.64 = bf16[4,2048,256]{2,1,0:T(8,128)(2,1)S(1)} custom-call(s32[16]{0:T(128)} %targets_hbm.1, s32[16]{0:T(128)} %pairs_hbm.1, bf16[4,4,64,2048]{3,2,1,0:T(8,128)(2,1)} %bitcast.1, bf16[256,2048]{1,0:T(8,128)(2,1)} %r_hbm.1, bf16[256,2048]{1,0:T(8,128)(2,1)} %l_hbm.1, f32[1024,1024]{1,0:T(8,128)} %integrals_hbm.1), custom_call_target="tpu_custom_call" | custom-call | tf_op jit(solution)/shard_map/pallas_call | solution.py:563
  141.9 2.0 %copy.8 = bf16[4,2048,256]{2,1,0:T(8,128)(2,1)} copy(bf16[4,2048,256]{2,1,0:T(8,128)(2,1)S(1)} %shard_map.64) | data formatting | bytes 8388608

commit v8 on v7

--- a/solution.py
+++ b/solution.py
@@ -331,8 +331,6 @@
     depart(LEFT, DOWN)
     launch(lambda: core_whole(LEFT))
     hop_right(nline - 1, 0)
-    if early:
-        early_mix()
     for h in range(1, nline - 1):
         spread_second(away, h)
     left_hop(1)
@@ -340,6 +338,8 @@
     hop_right(nline - 1, 1)
     for h in hops:
         spread_first(near, h)
+    if early:
+        early_mix()
     for h in hops:
         spread_third(away, h)
     load_r.wait()
@@ -425,7 +425,7 @@
             y_ref[s, :, :, at, :] = mixed.astype(jnp.bfloat16).reshape(npair, ntg, BLOCK, width)
             return carry
 
-        lax.fori_loop(0, late // BLOCK, chunk, 0)
+        lax.fori_loop(0, late // BLOCK, chunk, 0, unroll=True)
         for e in peers[::-1]:
             launch(lambda e=e: out_copy(s, e))
         out_local(s).start()

time: 144 us -> 144 us (level)
  no operation moved by 1% of the time
where the time goes in v8:
time: 144 us
  Pallas kernels  142 us (99%)
  local copies, waits for them, and re-layouts  2.02 us (1%)
    pallas_call x1, Pallas kernels, shards(): pl.pallas_call(functools.partial(kernel, npair, nline), out_shape=pltpu.V...  142 us

profile of v8, /device:TPU:0, one launch (start us, length us, event | category | flops | bytes accessed | tf_op | source)
XLA Modules:
  0.0 143.9 jit_solution(7729317315868109962)
XLA Ops:
  0.0 141.9 %shard_map.64 = bf16[4,2048,256]{2,1,0:T(8,128)(2,1)S(1)} custom-call(s32[16]{0:T(128)} %targets_hbm.1, s32[16]{0:T(128)} %pairs_hbm.1, bf16[4,4,64,2048]{3,2,1,0:T(8,128)(2,1)} %bitcast.1, bf16[256,2048]{1,0:T(8,128)(2,1)} %r_hbm.1, bf16[256,2048]{1,0:T(8,128)(2,1)} %l_hbm.1, f32[1024,1024]{1,0:T(8,128)} %integrals_hbm.1), custom_call_target="tpu_custom_call" | custom-call | tf_op jit(solution)/shard_map/pallas_call | solution.py:563
  141.9 2.0 %copy.8 = bf16[4,2048,256]{2,1,0:T(8,128)(2,1)} copy(bf16[4,2048,256]{2,1,0:T(8,128)(2,1)S(1)} %shard_map.64) | data formatting | bytes 8388608
